TPU v7x, 32 devices: a whole 2x2x4 slice. The times are simulated.
32 devices in a mesh: lat: 8 (over z, y), lon: 2 (over x), comp: 2 (over core).
Axes of the slice: x: 2, y: 2, z: 4, core: 2. Of those that a mesh axis runs over, the one named last changes fastest.
Arguments:
- atm_state: bfloat16 [192, 256, 384], P('lat', ('lon', 'comp')), may hold values from -6 to 6
- ocean_state: bfloat16 [192, 256, 256], P(('lat', 'comp'), 'lon'), may hold values from -6 to 6
- wet_mask: int32 [192, 256], P(('lat', 'comp'), 'lon'), may hold values 0 or 1
- legendre: bfloat16 [512, 384, 192], P(('lat', 'lon', 'comp')), may hold values from -4 to 4
- quad_weight: float32 [192], replicated, may hold values from 0.5 to 2
- spec_real: bfloat16 [384, 384], replicated, may hold values from -0.3125 to 0.3125
- spec_imag: bfloat16 [384, 384], replicated, may hold values from -0.3125 to 0.3125
- degree_gain: float32 [384], replicated, may hold values from 0.5 to 2
- atm_gain: float32 [2, 384], replicated, may hold values from 0.1 to 1.9
- atm_up: bfloat16 [384, 768], replicated, may hold values from -0.3125 to 0.3125
- atm_down: bfloat16 [768, 384], replicated, may hold values from -0.21875 to 0.21875
- atm_to_surface: bfloat16 [384, 32], replicated, may hold values from -0.3125 to 0.3125
- surface_to_atm: bfloat16 [32, 384], replicated, may hold values from -1 to 1
- ocean_to_surface: bfloat16 [256, 32], replicated, may hold values from -0.375 to 0.375
- surface_to_ocean: bfloat16 [32, 256], replicated, may hold values from -1 to 1
- ocean_kernel: bfloat16 [2, 7, 7, 256], replicated, may hold values from -0.875 to 0.875
- ocean_gain: float32 [2, 256], replicated, may hold values from 0.1 to 1.9
- ocean_up: bfloat16 [2, 256, 1024], replicated, may hold values from -0.375 to 0.375
- ocean_down: bfloat16 [2, 1024, 256], replicated, may hold values from -0.1875 to 0.1875
Outputs:
- atm_out: bfloat16 [192, 256, 384], P('lat', ('lon', 'comp'))
- ocean_out: bfloat16 [192, 256, 256], P(('lat', 'comp'), 'lon')
All inputs are finite; a program needn't handle non-finite values. No bound on the sum of `wet_mask` on one device may be relied on, other than what follows from the above.
Results may differ from a plain program's by a relative error of at most 0.01.
Values may be sent and summed in bfloat16 or wider, within the bound.
A program may use at most 128 MiB of HBM per device.

v0:
```python
import math

import jax
import jax.numpy as jnp
from jax import lax
from jax.sharding import PartitionSpec as P

MODES = 512
STENCIL_TAPS = 7
OCEAN_DILATION = 2


epsilon = 1e-05


def padded(block, sides, width):
    for axis, dim in sides:
        count = lax.axis_size(axis)
        forward = [(i, i + 1) for i in range(count - 1)]
        backward = [(target, source) for source, target in forward]
        low = lax.ppermute(
            lax.slice_in_dim(block, block.shape[dim] - width, None, axis=dim), axis, forward
        )
        high = lax.ppermute(lax.slice_in_dim(block, 0, width, axis=dim), axis, backward)
        block = jnp.concatenate([low, block, high], axis=dim)
    return block


def layer_norm(values, gain):
    centred = values - jnp.mean(values, axis=-1, keepdims=True)
    spread = jnp.mean(centred * centred, axis=-1, keepdims=True)
    return centred * lax.rsqrt(spread + epsilon) * gain


def wave_table(row_index, circle):
    longitude = jnp.arange(circle, dtype=jnp.int32)
    wavenumber = row_index // 2
    phases = wavenumber[:, None] * longitude[None, :] % circle
    angles = phases.astype(jnp.float32) * (2.0 * math.pi / circle)
    waves = jnp.where((row_index % 2 == 0)[:, None], jnp.cos(angles), -jnp.sin(angles))
    return (wavenumber, waves)


def forward_table(row_index, circle):
    wavenumber, waves = wave_table(row_index, circle)
    return (waves.T / math.sqrt(circle)).astype(jnp.bfloat16)


def inverse_table(row_index, circle):
    wavenumber, waves = wave_table(row_index, circle)
    factor = jnp.where(wavenumber == 0, 1.0, 2.0).astype(jnp.float32)
    return (waves * factor[:, None] / math.sqrt(circle)).astype(jnp.bfloat16)


def reorder_rows(total_rows, owned, lat_count, col_count):
    positions = jnp.arange(total_rows, dtype=jnp.int32)
    stride = lat_count * owned
    return (
        owned * (positions % stride // owned * col_count + positions // stride) + positions % owned
    )


def spectral_filter(gathered, table, quad_weight, spec_real, spec_imag, degree_gain):
    count = table.shape[0]
    lat_total = table.shape[2]
    channels = gathered.shape[2]
    split_parts = gathered.reshape(lat_total, count, 2, channels)
    weighted = (table.astype(jnp.float32) * (quad_weight / lat_total)).astype(jnp.bfloat16)
    coeffs = jnp.einsum(
        "mln,nmpc->mplc", weighted, split_parts, preferred_element_type=jnp.float32
    ).astype(jnp.bfloat16)
    real_part = coeffs[:, 0]
    imag_part = coeffs[:, 1]
    mixed_real = jnp.dot(real_part, spec_real, preferred_element_type=jnp.float32) - jnp.dot(
        imag_part, spec_imag, preferred_element_type=jnp.float32
    )
    mixed_imag = jnp.dot(real_part, spec_imag, preferred_element_type=jnp.float32) + jnp.dot(
        imag_part, spec_real, preferred_element_type=jnp.float32
    )
    scaled = (jnp.stack([mixed_real, mixed_imag], axis=1) * degree_gain[:, None]).astype(
        jnp.bfloat16
    )
    returned = jnp.einsum(
        "mln,mplc->nmpc", table, scaled, preferred_element_type=jnp.float32
    ).astype(jnp.bfloat16)
    return returned.reshape(lat_total, 2 * count, channels)


def ocean_block(padded_field, kernel, gain, up_weight, down_weight):
    stencil_reach = STENCIL_TAPS // 2 * OCEAN_DILATION
    tile_height = padded_field.shape[0] - 2 * stencil_reach
    tile_breadth = padded_field.shape[1] - 2 * stencil_reach
    stencil = jnp.zeros((tile_height, tile_breadth, padded_field.shape[2]), jnp.float32)
    for row_offset_tap in range(STENCIL_TAPS):
        for column_tap in range(STENCIL_TAPS):
            stencil_window = padded_field[
                row_offset_tap * OCEAN_DILATION : row_offset_tap * OCEAN_DILATION + tile_height,
                column_tap * OCEAN_DILATION : column_tap * OCEAN_DILATION + tile_breadth,
            ]
            stencil = stencil + stencil_window.astype(jnp.float32) * kernel[
                row_offset_tap, column_tap
            ].astype(jnp.float32)
    normed = layer_norm(stencil, gain).astype(jnp.bfloat16)
    hidden = jax.nn.gelu(jnp.dot(normed, up_weight, preferred_element_type=jnp.float32)).astype(
        jnp.bfloat16
    )
    centre = padded_field[
        stencil_reach : stencil_reach + tile_height, stencil_reach : stencil_reach + tile_breadth
    ]
    return (
        centre.astype(jnp.float32)
        + jnp.dot(hidden, down_weight, preferred_element_type=jnp.float32)
    ).astype(jnp.bfloat16)


def local(
    atm_state,
    ocean_state,
    wet_mask,
    legendre,
    quad_weight,
    spec_real,
    spec_imag,
    degree_gain,
    atm_gain,
    atm_up,
    atm_down,
    atm_to_surface,
    surface_to_atm,
    ocean_to_surface,
    surface_to_ocean,
    ocean_kernel,
    ocean_gain,
    ocean_up,
    ocean_down,
):
    lat_count = lax.axis_size("lat")
    col_count = lax.axis_size(("lon", "comp"))
    lat_dev, lon_dev, width = atm_state.shape
    sea_rows, sea_cols, sea_width = ocean_state.shape
    lat_total = lat_dev * lat_count
    circle = lon_dev * col_count
    total_rows = 2 * MODES
    owned = 2 * legendre.shape[0]
    natural = jnp.arange(total_rows, dtype=jnp.int32)
    wet = wet_mask.astype(jnp.float32)[:, :, None]
    ocean_flux = (
        jnp.dot(ocean_state, ocean_to_surface, preferred_element_type=jnp.float32) * wet
    ).astype(jnp.bfloat16)
    atm_flux = jnp.dot(atm_state, atm_to_surface, preferred_element_type=jnp.float32).astype(
        jnp.bfloat16
    )
    flux_here = lax.all_to_all(ocean_flux, "comp", split_axis=1, concat_axis=0, tiled=True)
    flux_sea = lax.all_to_all(atm_flux, "comp", split_axis=0, concat_axis=1, tiled=True)
    forced = atm_state.astype(jnp.float32) + jnp.dot(
        flux_here, surface_to_atm, preferred_element_type=jnp.float32
    )
    normed = layer_norm(forced, atm_gain[0]).astype(jnp.bfloat16)
    columns = lax.all_to_all(normed, ("lon", "comp"), split_axis=2, concat_axis=1, tiled=True)
    forward = forward_table(natural, circle)
    inverse = inverse_table(reorder_rows(total_rows, owned, lat_count, col_count), circle)
    spectrum = jnp.einsum(
        "anc,nr->arc", columns, forward, preferred_element_type=jnp.float32
    ).astype(jnp.bfloat16)
    gathered = lax.all_to_all(
        lax.all_to_all(spectrum, "lat", split_axis=1, concat_axis=0, tiled=True),
        ("lon", "comp"),
        split_axis=1,
        concat_axis=2,
        tiled=True,
    )
    filtered = spectral_filter(gathered, legendre, quad_weight, spec_real, spec_imag, degree_gain)
    returned = lax.all_to_all(
        lax.all_to_all(filtered, "lat", split_axis=0, concat_axis=1, tiled=True),
        ("lon", "comp"),
        split_axis=2,
        concat_axis=1,
        tiled=True,
    )
    spatial = jnp.einsum(
        "arc,rn->anc", returned, inverse, preferred_element_type=jnp.float32
    ).astype(jnp.bfloat16)
    spectral = lax.all_to_all(spatial, ("lon", "comp"), split_axis=1, concat_axis=2, tiled=True)
    mixed = forced + spectral.astype(jnp.float32)
    normed_two = layer_norm(mixed, atm_gain[1]).astype(jnp.bfloat16)
    hidden = jax.nn.gelu(jnp.dot(normed_two, atm_up, preferred_element_type=jnp.float32)).astype(
        jnp.bfloat16
    )
    atm_out = (mixed + jnp.dot(hidden, atm_down, preferred_element_type=jnp.float32)).astype(
        jnp.bfloat16
    )
    ocean_in = (
        ocean_state.astype(jnp.float32)
        + wet * jnp.dot(flux_sea, surface_to_ocean, preferred_element_type=jnp.float32)
    ).astype(jnp.bfloat16)
    stencil_reach = STENCIL_TAPS // 2 * OCEAN_DILATION
    padded_field = padded(ocean_in, ((("lat", "comp"), 0), ("lon", 1)), 2 * stencil_reach)
    first = ocean_block(padded_field, ocean_kernel[0], ocean_gain[0], ocean_up[0], ocean_down[0])
    row_global = (
        lax.axis_index(("lat", "comp")) * sea_rows
        - stencil_reach
        + jnp.arange(sea_rows + 2 * stencil_reach, dtype=jnp.int32)
    )
    col_global = (
        lax.axis_index("lon") * sea_cols
        - stencil_reach
        + jnp.arange(sea_cols + 2 * stencil_reach, dtype=jnp.int32)
    )
    inside = ((row_global >= 0) & (row_global < lat_total))[:, None] & (
        (col_global >= 0) & (col_global < circle)
    )[None, :]
    first = jnp.where(inside[:, :, None], first, jnp.zeros((), jnp.bfloat16))
    current = ocean_block(first, ocean_kernel[1], ocean_gain[1], ocean_up[1], ocean_down[1])
    ocean_out = jnp.where(wet_mask[:, :, None] == 1, current, ocean_state)
    return (atm_out, ocean_out)


def solution(mesh):
    placed = (
        P("lat", ("lon", "comp"), None),
        P(("lat", "comp"), "lon", None),
        P(("lat", "comp"), "lon"),
        P(("lat", "lon", "comp"), None, None),
        P(),
        P(),
        P(),
        P(),
        P(),
        P(),
        P(),
        P(),
        P(),
        P(),
        P(),
        P(),
        P(),
        P(),
        P(),
    )
    return jax.shard_map(
        local,
        mesh=mesh,
        in_specs=placed,
        out_specs=(P("lat", ("lon", "comp"), None), P(("lat", "comp"), "lon", None)),
        check_vma=False,
    )
```

profile of v0, /device:TPU:0, one launch (start us, length us, event | category | flops | bytes accessed | tf_op | source)
XLA Modules:
  0.0 632.4 jit_solution(10026933264612140607)
XLA Ops:
  22.5 16.9 %all-to-all-done.1 = bf16[4,2,73728]{2,1,0:T(2,128)(2,1)} async-done(((bf16[4,2,73728]{2,1,0:T(2,128)(2,1)}), bf16[4,2,73728]{2,1,0:T(2,128)(2,1)}, u32[]{:S(2)}, u32[]{:S(2)}) %all-to-all-start.1) | async-done | bytes 1179680 | tf_op jit(solution)/shard_map/all_to_all | solution.py:159
  47.2 6.6 %fusion.142 = f32[1024,2304]{0,1:S(1)} fusion(bf16[256,2304]{0,1:T(8,128)(2,1)S(1)} %bitcast.255, s32[1024]{0:T(1024)S(1)} %add_select_fusion.2, pred[1024]{0:T(1024)(128)(4,1)S(1)} %fusion.194), kind=kOutput, calls=%fused_computation.160 | convolution fusion | flops 1212678144 | bytes 10621952
  56.7 8.4 %copy.98 = bf16[24,1024,96]{2,0,1:T(8,128)(2,1)} copy(bf16[24,1024,96]{1,2,0:T(8,128)(2,1)} %convert_bitcast_fusion.1) | data formatting | bytes 9437184 | tf_op jit(solution)/shard_map/convert_element_type | solution.py:164
  65.0 6.4 %all-to-all-start.2 = ((bf16[24,1024,96]{2,0,1:T(8,128)(2,1)}), bf16[24,1024,96]{2,0,1:T(8,128)(2,1)}, u32[]{:S(2)}, u32[]{:S(2)}) async-start(bf16[24,1024,96]{2,0,1:T(8,128)(2,1)} %copy.98), calls=%async_computation.2 | async-start | bytes 12582912 | tf_op jit(solution)/shard_map/all_to_all | solution.py:166
  73.2 136.2 %all-to-all-done.2 = bf16[24,1024,96]{2,0,1:T(8,128)(2,1)} async-done(((bf16[24,1024,96]{2,0,1:T(8,128)(2,1)}), bf16[24,1024,96]{2,0,1:T(8,128)(2,1)}, u32[]{:S(2)}, u32[]{:S(2)}) %all-to-all-start.2) | async-done | bytes 4718624 | tf_op jit(solution)/shard_map/all_to_all | solution.py:166
  212.8 8.4 %copy.100 = bf16[8,24,128,96]{2,3,1,0:T(8,128)(2,1)} copy(bf16[8,24,128,96]{3,1,2,0:T(8,128)(2,1)} %bitcast.14) | data formatting | bytes 9437184 | tf_op jit(solution)/shard_map/all_to_all | solution.py:166
  221.1 8.4 %copy.101 = bf16[192,128,96]{2,0,1:T(8,128)(2,1)} copy(bf16[192,128,96]{1,2,0:T(8,128)(2,1)} %bitcast.250) | data formatting | bytes 9437184 | tf_op jit(solution)/shard_map/all_to_all | solution.py:166
  229.6 5.4 all-to-all-start.3
  242.7 63.0 %all-to-all-done.3 = bf16[192,128,96]{2,0,1:T(8,128)(2,1)} async-done(((bf16[192,128,96]{2,0,1:T(8,128)(2,1)}), bf16[192,128,96]{2,0,1:T(8,128)(2,1)}, u32[]{:S(2)}, u32[]{:S(2)}) %all-to-all-start.3) | async-done | bytes 4718624 | tf_op jit(solution)/shard_map/all_to_all | solution.py:165
  305.7 11.3 %copy.103 = bf16[192,32,4,96]{3,2,0,1:T(4,128)(2,1)} copy(bf16[192,32,4,96]{3,0,1,2:T(8,128)(2,1)} %bitcast.18) | data formatting | bytes 9437184 | tf_op jit(solution)/shard_map/all_to_all | solution.py:165
  317.0 11.0 %reshape.214 = bf16[192,16,2,384]{3,0,2,1:T(8,128)(2,1)} reshape(bf16[192,32,4,96]{3,2,0,1:T(4,128)(2,1)} %copy.103) | data formatting | bytes 9437184 | tf_op jit(solution)/shard_map/reshape | solution.py:67
  328.0 10.5 %convert_bitcast_fusion = bf16[16,2,384,384]{2,3,1,0:T(8,128)(2,1)} fusion(bf16[192,16,2,384]{3,0,2,1:T(8,128)(2,1)} %reshape.214, bf16[16,384,192]{1,2,0:T(8,128)(2,1)} %param.22, f32[192]{0:T(256)S(1)} %broadcast_multiply_fusion.4), kind=kOutput, calls=%fused_computation.16 | convolution fusion | flops 1820196864 | bytes 16515840 | tf_op jit(solution)/shard_map/mln,nmpc->mplc/dot_general | solution.py:69
  338.5 9.2 %fusion.27 = f32[16,384,384]{2,1,0:T(8,128)} fusion(bf16[16,2,384,384]{2,3,1,0:T(8,128)(2,1)} %convert_bitcast_fusion, bf16[384,384]{1,0:T(8,128)(2,1)S(1)} %copy-done.16), kind=kOutput, calls=%fused_computation.40 | convolution fusion | flops 1811939328 | bytes 14450688 | tf_op jit(solution)/shard_map/dot_general | solution.py:77
  350.8 8.2 %add_bitcast_fusion = f32[16,1,384,384]{3,2,0,1:T(8,128)} fusion(f32[16,384,384]{2,1,0:T(8,128)} %fusion.27, bf16[16,2,384,384]{2,3,1,0:T(8,128)(2,1)S(1)} %copy-done.1, bf16[384,384]{1,0:T(8,128)(2,1)S(1)} %copy-done.15), kind=kOutput, calls=%fused_computation.14 | convolution fusion | flops 1814298624 | bytes 23887872 | tf_op jit(solution)/shard_map/dot_general | solution.py:77
  359.0 5.5 subtract_bitcast_fusion
  364.5 9.7 %fusion.60 = bf16[16,2,384,192]{2,3,1,0:T(8,128)(2,1)S(1)} fusion(bf16[16,384,192]{1,2,0:T(8,128)(2,1)} %param.22, f32[16,1,384,384]{3,2,0,1:T(8,128)} %add_bitcast_fusion, f32[16,1,384,384]{3,2,0,1:T(8,128)} %subtract_bitcast_fusion, f32[384]{0:T(512)S(1)} %copy-done.31), kind=kOutput, calls=%fused_computation.75 | convolution fusion | flops 1828454400 | bytes 25953792 | tf_op jit(solution)/shard_map/mln,mplc->nmpc/dot_general | solution.py:83
  374.2 5.0 copy.109
  402.5 31.1 %fusion.231 = (f32[24,140]{1,0:T(8,128)S(1)}, f32[24,140,256]{2,1,0:T(8,128)}) fusion(f32[256]{0:T(256)S(1)} %bitcast.324, bf16[36,140,256]{2,1,0:T(8,128)(2,1)} %get-tuple-element.11, f32[256]{0:T(256)S(1)} %bitcast.325, bf16[36,152,256]{2,1,0:T(8,128)(2,1)S(1)} %pad_maximum_fusion, f32[256]{0:T(256)S(1)} %bitcast.326, f32[256]{0:T(256)S(1)} %bitcast.327, ...), kind=kLoop, calls=%fused_computation.381 | loop fusion | flops 126440160 | bytes 87799936 | tf_op jit(solution)/shard_map/reduce_sum | solution.py:30
  437.0 51.2 %all-to-all-done.4 = bf16[192,32,384]{2,1,0:T(8,128)(2,1)} async-done(((bf16[192,32,384]{2,1,0:T(8,128)(2,1)}), bf16[192,32,384]{2,1,0:T(8,128)(2,1)}, u32[]{:S(2)}, u32[]{:S(2)}) %all-to-all-start.4) | async-done | bytes 4718624 | tf_op jit(solution)/shard_map/all_to_all | solution.py:174
  488.2 5.4 copy.110
  493.7 7.0 %copy.111 = bf16[24,256,384]{1,0,2:T(8,128)(2,1)} copy(bf16[24,256,384]{2,1,0:T(8,128)(2,1)} %bitcast.249) | data formatting | bytes 9437184 | tf_op jit(solution)/shard_map/all_to_all | solution.py:174
  500.7 5.1 all-to-all-start.5
  505.8 8.9 %fusion.73 = bf16[24,140,256]{2,1,0:T(8,128)(2,1)} fusion(pred[24,140]{1,0:T(8,128)(4,1)S(1)} %broadcast_and_fusion, bf16[36,152,256]{2,1,0:T(8,128)(2,1)S(1)} %pad_maximum_fusion, f32[24,140,256]{2,1,0:T(8,128)} %get-tuple-element.7, f32[256]{0:T(256)} %bitcast.362, f32[24,140]{1,0:T(8,128)S(1)} %add_rsqrt_fusion, ...), kind=kOutput, calls=%fused_computation.93 | convolution fusion | flops 3561062400 | bytes 8059424 | tf_op jit(solution)/shard_map/dot_general | solution.py:112
  514.7 25.2 %fusion.229 = (f32[12,128]{1,0:T(8,128)S(1)}, f32[12,128,256]{2,1,0:T(8,128)S(1)}) fusion(f32[256]{0:T(256)S(1)} %bitcast.275, bf16[24,140,256]{2,1,0:T(8,128)(2,1)} %fusion.73, f32[256]{0:T(256)S(1)} %bitcast.276, f32[256]{0:T(256)S(1)} %bitcast.277, f32[256]{0:T(256)S(1)} %bitcast.278, f32[256]{0:T(256)S(1)} %bitcast.279, f32[256]{0:T(256)S(1)} %bitcast.280, ...), kind=kLoop, calls=%fused_computation.380 | loop fusion | flops 57801216 | bytes 40164352 | tf_op jit(solution)/shard_map/reduce_sum | solution.py:30
  540.4 19.3 %all-to-all-done.5 = bf16[24,256,384]{1,0,2:T(8,128)(2,1)} async-done(((bf16[24,256,384]{1,0,2:T(8,128)(2,1)}), bf16[24,256,384]{1,0,2:T(8,128)(2,1)}, u32[]{:S(2)}, u32[]{:S(2)}) %all-to-all-start.5) | async-done | bytes 4718624 | tf_op jit(solution)/shard_map/all_to_all | solution.py:173
  559.6 8.2 %copy.113 = bf16[24,4,256,96]{2,1,3,0:T(4,128)(2,1)} copy(bf16[24,4,256,96]{2,0,3,1:T(8,128)(2,1)} %bitcast.37) | data formatting | bytes 9437184 | tf_op jit(solution)/shard_map/all_to_all | solution.py:173
  567.8 8.7 %all_to_all.118 = bf16[24,1024,96]{1,2,0:T(8,128)(2,1)} reshape(bf16[24,4,256,96]{2,1,3,0:T(4,128)(2,1)} %copy.113) | data formatting | bytes 9437184 | tf_op jit(solution)/shard_map/all_to_all | solution.py:173
  576.5 7.9 %fusion.141 = f32[256,2304]{0,1:S(1)} fusion(bf16[1024,2304]{0,1:T(8,128)(2,1)} %bitcast.256, f32[1024]{0:T(1024)S(1)} %copy-done.22, s32[1024]{0:T(1024)S(1)} %copy-done.23, pred[1024]{0:T(1024)(128)(4,1)S(1)} %copy-done.32), kind=kOutput, calls=%fused_computation.159 | convolution fusion | flops 1212940288 | bytes 7087104
  586.4 4.7 all-to-all-start.6
  591.2 5.1 fusion.117
  596.3 15.0 %all-to-all-done.6 = bf16[24,256,96]{2,0,1:T(8,128)(2,1)} async-done(((bf16[24,256,96]{2,0,1:T(8,128)(2,1)}), bf16[24,256,96]{2,0,1:T(8,128)(2,1)}, u32[]{:S(2)}, u32[]{:S(2)}) %all-to-all-start.6) | async-done | bytes 1179680 | tf_op jit(solution)/shard_map/all_to_all | solution.py:183
  626.2 5.7 add_convert_fusion
  (142 shorter events, 92.0 us)
Async XLA Ops:
  0.6 625.6 %copy-start = (bf16[768,384]{1,0:T(8,128)(2,1)S(1)}, bf16[768,384]{1,0:T(8,128)(2,1)}, u32[]{:S(2)}) copy-start(bf16[768,384]{1,0:T(8,128)(2,1)} %param.29) | copy-start | bytes 1769476
  0.6 7.7 %copy-start.24 = (f32[2,384]{1,0:T(2,128)S(1)}, f32[2,384]{1,0:T(2,128)}, u32[]{:S(2)}) copy-start(f32[2,384]{1,0:T(2,128)} %param.27) | copy-start | bytes 9220
  0.7 8.3 %copy-start.19 = (bf16[32,384]{1,0:T(8,128)(2,1)S(1)}, bf16[32,384]{1,0:T(8,128)(2,1)}, u32[]{:S(2)}) copy-start(bf16[32,384]{1,0:T(8,128)(2,1)} %param.31) | copy-start | bytes 73732
  0.7 8.3 %copy-start.11 = (bf16[24,64,384]{2,1,0:T(8,128)(2,1)S(1)}, bf16[24,64,384]{2,1,0:T(8,128)(2,1)}, u32[]{:S(2)}) copy-start(bf16[24,64,384]{2,1,0:T(8,128)(2,1)} %param.19) | copy-start | bytes 3538948
  18.2 21.2 %all-to-all-start.1 = ((bf16[4,2,73728]{2,1,0:T(2,128)(2,1)}), bf16[4,2,73728]{2,1,0:T(2,128)(2,1)}, u32[]{:S(2)}, u32[]{:S(2)}) async-start(bf16[4,2,73728]{2,1,0:T(2,128)(2,1)} %reshape.338), calls=%async_computation.1 | async-start | bytes 2359296 | tf_op jit(solution)/shard_map/all_to_all | solution.py:159
  65.0 6.5 %copy-start.20 = (bf16[384,32]{0,1:T(8,128)(2,1)S(1)}, bf16[384,32]{0,1:T(8,128)(2,1)}, u32[]{:S(2)}) copy-start(bf16[384,32]{0,1:T(8,128)(2,1)} %param.30) | copy-start | bytes 73732
  65.0 144.4 %all-to-all-start.2 = ((bf16[24,1024,96]{2,0,1:T(8,128)(2,1)}), bf16[24,1024,96]{2,0,1:T(8,128)(2,1)}, u32[]{:S(2)}, u32[]{:S(2)}) async-start(bf16[24,1024,96]{2,0,1:T(8,128)(2,1)} %copy.98), calls=%async_computation.2 | async-start | bytes 12582912 | tf_op jit(solution)/shard_map/all_to_all | solution.py:166
  209.4 20.2 %all-to-all-start.7 = ((bf16[2,2,12288]{2,1,0:T(2,128)(2,1)}), bf16[2,2,12288]{2,1,0:T(2,128)(2,1)S(1)}, u32[]{:S(2)}, u32[]{:S(2)}) async-start(bf16[2,2,12288]{2,1,0:T(2,128)(2,1)} %reshape.340), calls=%async_computation.7 | async-start | bytes 196608 | tf_op jit(solution)/shard_map/all_to_all | solution.py:154
  229.6 11.7 %copy-start.28 = (f32[192]{0:T(256)S(1)}, f32[192]{0:T(256)}, u32[]{:S(2)}) copy-start(f32[192]{0:T(256)} %param.23) | copy-start | bytes 2308
  229.6 11.8 %copy-start.18 = (s32[12,128]{1,0:T(8,128)S(1)}, s32[12,128]{1,0:T(8,128)}, u32[]{:S(2)}) copy-start(s32[12,128]{1,0:T(8,128)} %param.21) | copy-start | bytes 18436
  229.6 76.1 %all-to-all-start.3 = ((bf16[192,128,96]{2,0,1:T(8,128)(2,1)}), bf16[192,128,96]{2,0,1:T(8,128)(2,1)}, u32[]{:S(2)}, u32[]{:S(2)}) async-start(bf16[192,128,96]{2,0,1:T(8,128)(2,1)} %copy.101), calls=%async_computation.3 | async-start | bytes 12582912 | tf_op jit(solution)/shard_map/all_to_all | solution.py:165
  235.0 6.9 %copy-start.17 = (bf16[2,7,7,256]{3,0,2,1:T(2,128)(2,1)S(1)}, bf16[2,7,7,256]{3,0,2,1:T(2,128)(2,1)}, u32[]{:S(2)}) copy-start(bf16[2,7,7,256]{3,0,2,1:T(2,128)(2,1)} %param.34) | copy-start | bytes 150532
  236.1 149.7 %copy-start.4 = (bf16[12,128,256]{2,1,0:T(8,128)(2,1)}, bf16[12,128,256]{2,1,0:T(8,128)(2,1)S(1)}, u32[]{:S(2)}) copy-start(bf16[12,128,256]{2,1,0:T(8,128)(2,1)S(1)} %add_convert_fusion.1) | copy-start | bytes 2359300
  236.1 149.6 %collective-permute-start.1 = (bf16[12,128,256]{2,1,0:T(8,128)(2,1)S(1)}, bf16[12,128,256]{2,1,0:T(8,128)(2,1)S(1)}, u32[]{:S(2)}, u32[]{:S(2)}) collective-permute-start(bf16[12,128,256]{2,1,0:T(8,128)(2,1)S(1)} %add_convert_fusion.1), channel_id=1, source_target_pairs={{1,0},{4,1},{5,4},{8,5},{9,8},{12,9},{13,12},{16,13},{17,16},{20,1... | collective-permute-start | bytes 2359304 | tf_op jit(solution)/shard_map/ppermute | solution.py:24
  237.4 148.3 %collective-permute-start = (bf16[12,128,256]{2,1,0:T(8,128)(2,1)S(1)}, bf16[12,128,256]{2,1,0:T(8,128)(2,1)S(1)}, u32[]{:S(2)}, u32[]{:S(2)}) collective-permute-start(bf16[12,128,256]{2,1,0:T(8,128)(2,1)S(1)} %add_convert_fusion.1), channel_id=1, source_target_pairs={{0,1},{1,4},{4,5},{5,8},{8,9},{9,12},{12,13},{13,16},{16,17},{17,2... | collective-permute-start | bytes 2359304 | tf_op jit(solution)/shard_map/ppermute | solution.py:21
  328.0 10.5 %copy-start.16 = (bf16[384,384]{1,0:T(8,128)(2,1)S(1)}, bf16[384,384]{1,0:T(8,128)(2,1)}, u32[]{:S(2)}) copy-start(bf16[384,384]{1,0:T(8,128)(2,1)} %param.25) | copy-start | bytes 884740
  338.5 9.2 %copy-start.1 = (bf16[16,2,384,384]{2,3,1,0:T(8,128)(2,1)S(1)}, bf16[16,2,384,384]{2,3,1,0:T(8,128)(2,1)}, u32[]{:S(2)}) copy-start(bf16[16,2,384,384]{2,3,1,0:T(8,128)(2,1)} %convert_bitcast_fusion) | copy-start | bytes 28311556
  338.5 9.2 %copy-start.15 = (bf16[384,384]{1,0:T(8,128)(2,1)S(1)}, bf16[384,384]{1,0:T(8,128)(2,1)}, u32[]{:S(2)}) copy-start(bf16[384,384]{1,0:T(8,128)(2,1)} %param.24) | copy-start | bytes 884740
  379.2 109.0 %all-to-all-start.4 = ((bf16[192,32,384]{2,1,0:T(8,128)(2,1)}), bf16[192,32,384]{2,1,0:T(8,128)(2,1)}, u32[]{:S(2)}, u32[]{:S(2)}) async-start(bf16[192,32,384]{2,1,0:T(8,128)(2,1)} %copy.109), calls=%async_computation.4 | async-start | bytes 9437184 | tf_op jit(solution)/shard_map/all_to_all | solution.py:174
  383.8 7.9 %copy-start.27 = (f32[2,256]{1,0:T(2,128)S(1)}, f32[2,256]{1,0:T(2,128)}, u32[]{:S(2)}) copy-start(f32[2,256]{1,0:T(2,128)} %param.35) | copy-start | bytes 6148
  385.7 10.5 %copy-start.7 = (bf16[12,128,256]{2,1,0:T(8,128)(2,1)}, bf16[12,128,256]{2,1,0:T(8,128)(2,1)S(1)}, u32[]{:S(2)}) copy-start(bf16[12,128,256]{2,1,0:T(8,128)(2,1)S(1)} %collective-permute-done.1) | copy-start | bytes 2359300
  385.7 10.5 %copy-start.9 = (bf16[12,128,256]{2,1,0:T(8,128)(2,1)}, bf16[12,128,256]{2,1,0:T(8,128)(2,1)S(1)}, u32[]{:S(2)}) copy-start(bf16[12,128,256]{2,1,0:T(8,128)(2,1)S(1)} %collective-permute-done) | copy-start | bytes 2359300
  385.8 10.4 %collective-permute-start.3 = (bf16[36,12,256]{2,1,0:T(8,128)(2,1)S(1)}, bf16[36,12,256]{2,1,0:T(8,128)(2,1)S(1)}, u32[]{:S(2)}, u32[]{:S(2)}) collective-permute-start(bf16[36,12,256]{2,1,0:T(8,128)(2,1)S(1)} %get-tuple-element.13), channel_id=1, source_target_pairs={{2,0},{3,1},{6,4},{7,5},{10,8},{11,9},{14,12},{15,13},{18,16},{19,... | collective-permute-start | bytes 663560 | tf_op jit(solution)/shard_map/ppermute | solution.py:24
  387.1 10.3 %collective-permute-start.2 = (bf16[36,12,256]{2,1,0:T(8,128)(2,1)S(1)}, bf16[36,12,256]{2,1,0:T(8,128)(2,1)S(1)}, u32[]{:S(2)}, u32[]{:S(2)}) collective-permute-start(bf16[36,12,256]{2,1,0:T(8,128)(2,1)S(1)} %get-tuple-element.12), channel_id=1, source_target_pairs={{0,2},{1,3},{4,6},{5,7},{8,10},{9,11},{12,14},{13,15},{16,18},{17,... | collective-permute-start | bytes 663560 | tf_op jit(solution)/shard_map/ppermute | solution.py:21
  392.3 7.7 %copy-start.5 = (bf16[12,128,256]{2,1,0:T(8,128)(2,1)S(1)}, bf16[12,128,256]{2,1,0:T(8,128)(2,1)}, u32[]{:S(2)}) copy-start(bf16[12,128,256]{2,1,0:T(8,128)(2,1)} %copy-done.4) | copy-start | bytes 2359300
  500.7 58.9 %all-to-all-start.5 = ((bf16[24,256,384]{1,0,2:T(8,128)(2,1)}), bf16[24,256,384]{1,0,2:T(8,128)(2,1)}, u32[]{:S(2)}, u32[]{:S(2)}) async-start(bf16[24,256,384]{1,0,2:T(8,128)(2,1)} %copy.111), calls=%async_computation.5 | async-start | bytes 9437184 | tf_op jit(solution)/shard_map/all_to_all | solution.py:173
  567.8 8.7 %copy-start.22 = (f32[1024]{0:T(1024)S(1)}, f32[1024]{0:T(1024)}, u32[]{:S(2)}) copy-start(f32[1024]{0:T(1024)} %compare_select_fusion) | copy-start | bytes 12292
  567.8 8.7 %copy-start.23 = (s32[1024]{0:T(1024)S(1)}, s32[1024]{0:T(1024)}, u32[]{:S(2)}) copy-start(s32[1024]{0:T(1024)} %add_select_fusion.4) | copy-start | bytes 12292
  567.8 8.7 %copy-start.32 = (pred[1024]{0:T(1024)(128)(4,1)S(1)}, pred[1024]{0:T(1024)(128)(4,1)}, u32[]{:S(2)}) copy-start(pred[1024]{0:T(1024)(128)(4,1)} %fusion.193) | copy-start | bytes 3076
  584.6 6.6 %copy-start.26 = (pred[12,128]{1,0:T(8,128)(4,1)S(1)}, pred[12,128]{1,0:T(8,128)(4,1)}, u32[]{:S(2)}) copy-start(pred[12,128]{1,0:T(8,128)(4,1)} %broadcast_compare_fusion) | copy-start | bytes 4612
  584.6 6.6 %copy-start.29 = (f32[1,256]{1,0:T(1,128)S(1)}, f32[1,256]{1,0:T(1,128)}, u32[]{:S(2)}) copy-start(f32[1,256]{1,0:T(1,128)} %get-tuple-element.114) | copy-start | bytes 3076
  586.4 24.8 %all-to-all-start.6 = ((bf16[24,256,96]{2,0,1:T(8,128)(2,1)}), bf16[24,256,96]{2,0,1:T(8,128)(2,1)}, u32[]{:S(2)}, u32[]{:S(2)}) async-start(bf16[24,256,96]{2,0,1:T(8,128)(2,1)} %copy.114), calls=%async_computation.6 | async-start | bytes 3145728 | tf_op jit(solution)/shard_map/all_to_all | solution.py:183
  (12 other events, 49.5 us)
where the time goes:
time: 643 us; the launch traced here: 632 us
  waiting for transfers between devices  307 us (48%)
  local copies, waits for them, and re-layouts  114 us (18%)
  matrix products  83.7 us (13%)
  other arithmetic  78 us (12%)
  starting transfers between devices  44.3 us (7%)
    all_to_all x1, waiting for transfers between devices, local(): lax.all_to_all(spectrum, 'lat', split_axis=1, concat_axis=0, tiled=True)  136 us
    all_to_all x1, waiting for transfers between devices, local(): lax.all_to_all(lax.all_to_all(spectrum, 'lat', split_axis=1, concat_axis=...  63 us
    reduce_sum x3, other arithmetic, layer_norm(): centred = values - jnp.mean(values, axis=-1, keepdims=True)  58.3 us
    all_to_all x1, waiting for transfers between devices, local(): lax.all_to_all(filtered, 'lat', split_axis=0, concat_axis=1, tiled=True)  51.2 us
    all_to_all x1, waiting for transfers between devices, local(): lax.all_to_all(lax.all_to_all(filtered, 'lat', split_axis=0, concat_axis=...  19.3 us
    all_to_all x2, local copies, waits for them, and re-layouts, local(): lax.all_to_all(lax.all_to_all(filtered, 'lat', split_axis=0, concat_axis=...  16.9 us
    all_to_all x1, waiting for transfers between devices, local(): lax.all_to_all(normed, ('lon', 'comp'), split_axis=2, concat_axis=1, tile...  16.9 us
    all_to_all x2, local copies, waits for them, and re-layouts, local(): lax.all_to_all(spectrum, 'lat', split_axis=1, concat_axis=0, tiled=True)  16.8 us
  transfers between devices with their start and end apart: 11, of which 8 were waited for; matrix products, arithmetic and copies ran while one was open for 28% of the time, Pallas kernels for 0%

commit v1 on v0

--- a/solution.py
+++ b/solution.py
@@ -8,6 +8,8 @@
 MODES = 512
 STENCIL_TAPS = 7
 OCEAN_DILATION = 2
+COLUMNS = ("lon", "comp")
+EVERY = ("lat", "lon", "comp")
 
 
 epsilon = 1e-05
@@ -84,6 +86,127 @@
         "mln,mplc->nmpc", table, scaled, preferred_element_type=jnp.float32
     ).astype(jnp.bfloat16)
     return returned.reshape(lat_total, 2 * count, channels)
+
+
+def folds(circle, lat_dev, col_count, devices):
+    return (
+        MODES == 2 * circle
+        and lat_dev % col_count == 0
+        and devices % 4 == 0
+        and (circle // 2) % devices == 0
+        and (MODES // devices) % 4 == 0
+    )
+
+
+def folded_waves(circle):
+    longitude = jnp.arange(circle, dtype=jnp.int32)
+    row_index = jnp.arange(circle, dtype=jnp.int32)
+    wavenumber = jnp.where(row_index == 1, circle // 2, row_index // 2)
+    phases = wavenumber[:, None] * longitude[None, :] % circle
+    angles = phases.astype(jnp.float32) * (2.0 * math.pi / circle)
+    cosine = ((row_index % 2 == 0) | (row_index == 1))[:, None]
+    return jnp.where(cosine, jnp.cos(angles), -jnp.sin(angles)) / math.sqrt(circle)
+
+
+def folded_operators(table, quad_weight, degree_gain):
+    devices = lax.axis_size(EVERY)
+    me = lax.axis_index(EVERY)
+    count, degrees, lat_total = table.shape
+    group = devices // 4
+    part = count // 4
+    family = me // group
+    scaled = (table.astype(jnp.float32) * degree_gain[:, None]).astype(jnp.bfloat16)
+    operators = jnp.einsum("mlt,mlu->mtu", table, scaled, preferred_element_type=jnp.float32)
+    operators = operators * (quad_weight / lat_total)
+    first_scale = jnp.where(me == 0, 0.5, 1.0).astype(jnp.float32)
+    scales = jnp.where(jnp.arange(count) == 0, first_scale, 1.0)
+    operators = (operators * scales[:, None, None]).astype(jnp.bfloat16)
+    turn = []
+    for base in (group, 3 * group):
+        for i in range(group):
+            turn.append((base + (i + 1) % group, base + i))
+    rotated = lax.ppermute(operators[:1], EVERY, turn)
+    mirrored = jnp.concatenate([rotated, jnp.flip(operators[1:], axis=0)], axis=0)
+    ordered = jnp.where(family % 2 == 1, mirrored, operators)
+    received = []
+    for step in range(4):
+        pairs = []
+        for source in range(devices):
+            kind, place = source // group, source % group
+            place = group - 1 - place if kind % 2 else place
+            pairs.append((source, 4 * place + (step + kind) % 4))
+        piece = lax.dynamic_slice_in_dim(ordered, (step + family) % 4 * part, part, axis=0)
+        received.append(lax.ppermute(piece, EVERY, pairs).astype(jnp.float32))
+    even = received[0] + received[2]
+    odd = received[1] + received[3]
+    direct = jnp.where(me % 2 == 0, even, odd)
+    mirror = jnp.where(me % 2 == 0, odd, even)
+    lone = ((me == 0) & (jnp.arange(part) == 0))[:, None, None]
+    both = direct + mirror
+    gap = jnp.where(lone, 0.0, direct - mirror)
+    top = jnp.concatenate([jnp.where(lone, direct, both), -gap], axis=2)
+    bottom = jnp.concatenate([gap, jnp.where(lone, mirror, both)], axis=2)
+    return (2.0 * top).astype(jnp.bfloat16), (2.0 * bottom).astype(jnp.bfloat16)
+
+
+def folded_spectral(normed, legendre, quad_weight, spec_real, spec_imag, degree_gain, circle):
+    width = normed.shape[2]
+    top, bottom = folded_operators(legendre, quad_weight, degree_gain)
+    slots = top.shape[0]
+    waves = folded_waves(circle).astype(jnp.bfloat16)
+    columns = lax.all_to_all(normed, COLUMNS, split_axis=0, concat_axis=1, tiled=True)
+    spectrum = jnp.einsum(
+        "rn,tnc->trc", waves, columns, preferred_element_type=jnp.float32
+    ).astype(jnp.bfloat16)
+    gathered = lax.all_to_all(spectrum, EVERY, split_axis=1, concat_axis=0, tiled=True)
+    lat_total = gathered.shape[0]
+    channels = jnp.concatenate([spec_real, spec_imag], axis=1)
+    turned = gathered.reshape(lat_total, slots, 2, width).transpose(1, 2, 0, 3)
+    mixed = jnp.dot(turned, channels, preferred_element_type=jnp.float32).astype(jnp.bfloat16)
+    upper = jnp.concatenate([mixed[:, 0, :, :width], mixed[:, 1, :, width:]], axis=1)
+    lower = jnp.concatenate([mixed[:, 0, :, width:], mixed[:, 1, :, :width]], axis=1)
+    cosine = jnp.einsum("stu,suc->stc", top, upper, preferred_element_type=jnp.float32)
+    sine = jnp.einsum("stu,suc->stc", bottom, lower, preferred_element_type=jnp.float32)
+    filtered = jnp.stack([cosine, sine], axis=1).astype(jnp.bfloat16)
+    filtered = filtered.reshape(2 * slots, lat_total, width).transpose(1, 0, 2)
+    returned = lax.all_to_all(filtered, EVERY, split_axis=0, concat_axis=1, tiled=True)
+    spatial = jnp.einsum(
+        "rn,trc->tnc", waves, returned, preferred_element_type=jnp.float32
+    ).astype(jnp.bfloat16)
+    return lax.all_to_all(spatial, COLUMNS, split_axis=1, concat_axis=0, tiled=True)
+
+
+def plain_spectral(normed, legendre, quad_weight, spec_real, spec_imag, degree_gain, circle):
+    lat_count = lax.axis_size("lat")
+    col_count = lax.axis_size(("lon", "comp"))
+    total_rows = 2 * MODES
+    owned = 2 * legendre.shape[0]
+    natural = jnp.arange(total_rows, dtype=jnp.int32)
+    columns = lax.all_to_all(normed, ("lon", "comp"), split_axis=2, concat_axis=1, tiled=True)
+    forward = forward_table(natural, circle)
+    inverse = inverse_table(reorder_rows(total_rows, owned, lat_count, col_count), circle)
+    spectrum = jnp.einsum(
+        "anc,nr->arc", columns, forward, preferred_element_type=jnp.float32
+    ).astype(jnp.bfloat16)
+    gathered = lax.all_to_all(
+        lax.all_to_all(spectrum, "lat", split_axis=1, concat_axis=0, tiled=True),
+        ("lon", "comp"),
+        split_axis=1,
+        concat_axis=2,
+        tiled=True,
+    )
+    filtered = spectral_filter(gathered, legendre, quad_weight, spec_real, spec_imag, degree_gain)
+    returned = lax.all_to_all(
+        lax.all_to_all(filtered, "lat", split_axis=0, concat_axis=1, tiled=True),
+        ("lon", "comp"),
+        split_axis=2,
+        concat_axis=1,
+        tiled=True,
+    )
+    spatial = jnp.einsum(
+        "arc,rn->anc", returned, inverse, preferred_element_type=jnp.float32
+    ).astype(jnp.bfloat16)
+    return lax.all_to_all(spatial, ("lon", "comp"), split_axis=1, concat_axis=2, tiled=True)
 
 
 def ocean_block(padded_field, kernel, gain, up_weight, down_weight):
@@ -134,15 +257,9 @@
     ocean_up,
     ocean_down,
 ):
-    lat_count = lax.axis_size("lat")
-    col_count = lax.axis_size(("lon", "comp"))
+    col_count = lax.axis_size(COLUMNS)
     lat_dev, lon_dev, width = atm_state.shape
-    sea_rows, sea_cols, sea_width = ocean_state.shape
-    lat_total = lat_dev * lat_count
     circle = lon_dev * col_count
-    total_rows = 2 * MODES
-    owned = 2 * legendre.shape[0]
-    natural = jnp.arange(total_rows, dtype=jnp.int32)
     wet = wet_mask.astype(jnp.float32)[:, :, None]
     ocean_flux = (
         jnp.dot(ocean_state, ocean_to_surface, preferred_element_type=jnp.float32) * wet
@@ -156,31 +273,14 @@
         flux_here, surface_to_atm, preferred_element_type=jnp.float32
     )
     normed = layer_norm(forced, atm_gain[0]).astype(jnp.bfloat16)
-    columns = lax.all_to_all(normed, ("lon", "comp"), split_axis=2, concat_axis=1, tiled=True)
-    forward = forward_table(natural, circle)
-    inverse = inverse_table(reorder_rows(total_rows, owned, lat_count, col_count), circle)
-    spectrum = jnp.einsum(
-        "anc,nr->arc", columns, forward, preferred_element_type=jnp.float32
-    ).astype(jnp.bfloat16)
-    gathered = lax.all_to_all(
-        lax.all_to_all(spectrum, "lat", split_axis=1, concat_axis=0, tiled=True),
-        ("lon", "comp"),
-        split_axis=1,
-        concat_axis=2,
-        tiled=True,
-    )
-    filtered = spectral_filter(gathered, legendre, quad_weight, spec_real, spec_imag, degree_gain)
-    returned = lax.all_to_all(
-        lax.all_to_all(filtered, "lat", split_axis=0, concat_axis=1, tiled=True),
-        ("lon", "comp"),
-        split_axis=2,
-        concat_axis=1,
-        tiled=True,
-    )
-    spatial = jnp.einsum(
-        "arc,rn->anc", returned, inverse, preferred_element_type=jnp.float32
-    ).astype(jnp.bfloat16)
-    spectral = lax.all_to_all(spatial, ("lon", "comp"), split_axis=1, concat_axis=2, tiled=True)
+    run_spectral = (
+        folded_spectral
+        if folds(circle, lat_dev, col_count, lax.axis_size(EVERY))
+        else plain_spectral
+    )
+    spectral = run_spectral(
+        normed, legendre, quad_weight, spec_real, spec_imag, degree_gain, circle
+    )
     mixed = forced + spectral.astype(jnp.float32)
     normed_two = layer_norm(mixed, atm_gain[1]).astype(jnp.bfloat16)
     hidden = jax.nn.gelu(jnp.dot(normed_two, atm_up, preferred_element_type=jnp.float32)).astype(
@@ -194,23 +294,11 @@
         + wet * jnp.dot(flux_sea, surface_to_ocean, preferred_element_type=jnp.float32)
     ).astype(jnp.bfloat16)
     stencil_reach = STENCIL_TAPS // 2 * OCEAN_DILATION
-    padded_field = padded(ocean_in, ((("lat", "comp"), 0), ("lon", 1)), 2 * stencil_reach)
-    first = ocean_block(padded_field, ocean_kernel[0], ocean_gain[0], ocean_up[0], ocean_down[0])
-    row_global = (
-        lax.axis_index(("lat", "comp")) * sea_rows
-        - stencil_reach
-        + jnp.arange(sea_rows + 2 * stencil_reach, dtype=jnp.int32)
-    )
-    col_global = (
-        lax.axis_index("lon") * sea_cols
-        - stencil_reach
-        + jnp.arange(sea_cols + 2 * stencil_reach, dtype=jnp.int32)
-    )
-    inside = ((row_global >= 0) & (row_global < lat_total))[:, None] & (
-        (col_global >= 0) & (col_global < circle)
-    )[None, :]
-    first = jnp.where(inside[:, :, None], first, jnp.zeros((), jnp.bfloat16))
-    current = ocean_block(first, ocean_kernel[1], ocean_gain[1], ocean_up[1], ocean_down[1])
+    sides = ((("lat", "comp"), 0), ("lon", 1))
+    current = ocean_in
+    for k in range(2):
+        field = padded(current, sides, stencil_reach)
+        current = ocean_block(field, ocean_kernel[k], ocean_gain[k], ocean_up[k], ocean_down[k])
     ocean_out = jnp.where(wet_mask[:, :, None] == 1, current, ocean_state)
     return (atm_out, ocean_out)
 

time: 643 us -> 263 us (0.41); the launches traced: 632 us -> 261 us
  waiting for transfers between devices: 307 us -> 44.5 us
  local copies, waits for them, and re-layouts: 114 us -> 32.7 us
  matrix products: 83.7 us -> 32.6 us
  starting transfers between devices: 44.3 us -> 87.8 us
  other arithmetic: 78 us -> 61.7 us
    all_to_all x6 -> x5, waiting for transfers between devices: 302 us -> 41.3 us  [the longest x1 21.9 us: folded_spectral(): lax.all_to_all(spectrum, EVERY, split_axis=1, concat_axis=0, tiled=True)]
    all_to_all x10 -> x2, local copies, waits for them, and re-layouts: 63.7 us -> 2.96 us  [the longest x1 1.56 us: folded_spectral(): lax.all_to_all(spatial, COLUMNS, split_axis=1, concat_axis=0, tiled=True)]
    dot_general x6, matrix products: 46.2 us -> 12.6 us  [the longest x1 3.49 us: folded_operators(): jnp.einsum('mlt,mlu->mtu', table, scaled, preferred_element_type=jnp.floa...]
    reduce_sum x3, other arithmetic: 58.3 us -> 39.5 us  [layer_norm(): centred = values - jnp.mean(values, axis=-1, keepdims=True)]
    ppermute x0 -> x5, starting transfers between devices: none -> 17.8 us  [the longest x4 16.5 us: folded_operators(): received.append(lax.ppermute(piece, EVERY, pairs).astype(jnp.float32))]
    ppermute x2 -> x4, starting transfers between devices: 7.83 us -> 22.9 us  [padded(): lax.ppermute(lax.slice_in_dim(block, block.shape[dim] - width, None, axis...]
    unnamed x2 -> x0, matrix products: 14.5 us -> none
    reshape x2, local copies, waits for them, and re-layouts: 16 us -> 6.06 us  [folded_spectral(): turned = gathered.reshape(lat_total, slots, 2, width).transpose(1, 2, 0, 3)]
  transfers between devices with their start and end apart: 11 -> 19, of which waited for: 8 -> 4; matrix products, arithmetic and copies ran while one was open for 28% -> 35% of each run, Pallas kernels for 0% -> 0%
where the time goes in v1:
time: 263 us; the launch traced here: 261 us
  starting transfers between devices  87.8 us (33%)
  other arithmetic  61.7 us (23%)
  waiting for transfers between devices  44.5 us (17%)
  local copies, waits for them, and re-layouts  32.7 us (12%)
  matrix products  32.6 us (12%)
    reduce_sum x3, other arithmetic, layer_norm(): centred = values - jnp.mean(values, axis=-1, keepdims=True)  39.5 us
    ppermute x4, starting transfers between devices, padded(): lax.ppermute(lax.slice_in_dim(block, block.shape[dim] - width, None, axis...  22.9 us
    all_to_all x1, waiting for transfers between devices, folded_spectral(): lax.all_to_all(spectrum, EVERY, split_axis=1, concat_axis=0, tiled=True)  21.9 us
    all_to_all x1, starting transfers between devices, folded_spectral(): lax.all_to_all(filtered, EVERY, split_axis=0, concat_axis=1, tiled=True)  19.7 us
    ppermute x4, starting transfers between devices, folded_operators(): received.append(lax.ppermute(piece, EVERY, pairs).astype(jnp.float32))  16.5 us
    all_to_all x1, waiting for transfers between devices, folded_spectral(): lax.all_to_all(spatial, COLUMNS, split_axis=1, concat_axis=0, tiled=True)  14.8 us
    dot_general x2, matrix products, ocean_block(): jnp.dot(hidden, down_weight, preferred_element_type=jnp.float32)  9.23 us
    unnamed x158, local copies, waits for them, and re-layouts  7.97 us
  transfers between devices with their start and end apart: 19, of which 4 were waited for; matrix products, arithmetic and copies ran while one was open for 35% of the time, Pallas kernels for 0%

profile of v1, /device:TPU:0, one launch (start us, length us, event | category | flops | bytes accessed | tf_op | source)
XLA Modules:
  0.0 261.4 jit_solution(8465687373026479112)
XLA Ops:
  4.4 3.3 %all-to-all-start = ((bf16[2,2,12288]{2,1,0:T(2,128)(2,1)}), bf16[2,2,12288]{2,1,0:T(2,128)(2,1)S(1)}, u32[]{:S(2)}, u32[]{:S(2)}) async-start(bf16[2,2,12288]{2,1,0:T(2,128)(2,1)} %reshape.226), calls=%async_computation | async-start | bytes 196608 | tf_op jit(solution)/shard_map/all_to_all | solution.py:270
  7.8 3.5 %fusion.90 = bf16[16,192,192]{2,1,0:T(8,128)(2,1)S(1)} fusion(f32[16]{0:T(128)S(1)} %compare_select_fusion, f32[192]{0:T(256)S(1)} %broadcast_multiply_fusion.4, bf16[16,384,192]{1,2,0:T(8,128)(2,1)} %param.22, f32[384]{0:T(512)S(1)} %copy-done.72), kind=kOutput, calls=%fused_computation.113 | convolution fusion | flops 458293248 | bytes 3541312 | tf_op jit(solution)/shard_map/mlt,mlu->mtu/dot_general | solution.py:119
  14.4 3.3 %all-to-all-start.5 = ((bf16[2,2,12288]{2,1,0:T(2,128)(2,1)}), bf16[2,2,12288]{2,1,0:T(2,128)(2,1)S(1)}, u32[]{:S(2)}, u32[]{:S(2)}) async-start(bf16[2,2,12288]{2,1,0:T(2,128)(2,1)} %reshape.228), calls=%async_computation.5 | async-start | bytes 196608 | tf_op jit(solution)/shard_map/all_to_all | solution.py:271
  23.8 4.5 %all-to-all-start.1 = ((bf16[24,64,384]{2,1,0:T(8,128)(2,1)}), bf16[24,64,384]{2,1,0:T(8,128)(2,1)}, u32[]{:S(2)}, u32[]{:S(2)}) async-start(bf16[24,64,384]{2,1,0:T(8,128)(2,1)} %multiply_convert_fusion.4), calls=%async_computation.1 | async-start | bytes 2359296 | tf_op jit(solution)/shard_map/all_to_all | solution.py:157
  32.8 3.8 %collective-permute-start.5 = (bf16[6,128,256]{2,1,0:T(8,128)(2,1)}, bf16[6,128,256]{2,1,0:T(8,128)(2,1)}, u32[]{:S(2)}, u32[]{:S(2)}) collective-permute-start(bf16[6,128,256]{2,1,0:T(8,128)(2,1)} %get-tuple-element.34), channel_id=1, source_target_pairs={{0,1},{1,4},{4,5},{5,8},{8,9},{9,12},{12,13},{13,16},{16,17},{17,2... | collective-permute-start | bytes 1179656 | tf_op jit(solution)/shard_map/ppermute | solution.py:23
  42.9 2.7 %rev.4 = bf16[15,192,192]{2,1,0:T(8,128)(2,1)} reverse(bf16[15,192,192]{2,1,0:T(8,128)(2,1)} %slice.969), dimensions={0} | reverse | bytes 2211840 | tf_op jit(solution)/shard_map/jit(_flip)/rev | solution.py:129
  50.0 4.8 %collective-permute-start.7 = (bf16[24,6,256]{2,1,0:T(8,128)(2,1)S(1)}, bf16[24,6,256]{2,1,0:T(8,128)(2,1)S(1)}, u32[]{:S(2)}, u32[]{:S(2)}) collective-permute-start(bf16[24,6,256]{2,1,0:T(8,128)(2,1)S(1)} %get-tuple-element.26), channel_id=1, source_target_pairs={{0,2},{1,3},{4,6},{5,7},{8,10},{9,11},{12,14},{13,15},{16,18},{17,... | collective-permute-start | bytes 221192 | tf_op jit(solution)/shard_map/ppermute | solution.py:23
  57.2 4.5 %collective-permute-start.4 = (bf16[4,192,192]{2,1,0:T(8,128)(2,1)}, bf16[4,192,192]{2,1,0:T(8,128)(2,1)}, u32[]{:S(2)}, u32[]{:S(2)}) collective-permute-start(bf16[4,192,192]{2,1,0:T(8,128)(2,1)} %get-tuple-element.29), channel_id=1, source_target_pairs={{0,3},{1,7},{2,11},{3,15},{4,19},{5,23},{6,27},{7,31},{8,28},{9,24... | collective-permute-start | bytes 884744 | tf_op jit(solution)/shard_map/ppermute | solution.py:139
  61.8 4.2 %collective-permute-start.3 = (bf16[4,192,192]{2,1,0:T(8,128)(2,1)}, bf16[4,192,192]{2,1,0:T(8,128)(2,1)}, u32[]{:S(2)}, u32[]{:S(2)}) collective-permute-start(bf16[4,192,192]{2,1,0:T(8,128)(2,1)} %get-tuple-element.30), channel_id=1, source_target_pairs={{0,1},{1,5},{2,9},{3,13},{4,17},{5,21},{6,25},{7,29},{8,30},{9,26}... | collective-permute-start | bytes 884744 | tf_op jit(solution)/shard_map/ppermute | solution.py:139
  65.9 3.4 %collective-permute-start.2 = (bf16[4,192,192]{2,1,0:T(8,128)(2,1)}, bf16[4,192,192]{2,1,0:T(8,128)(2,1)}, u32[]{:S(2)}, u32[]{:S(2)}) collective-permute-start(bf16[4,192,192]{2,1,0:T(8,128)(2,1)} %get-tuple-element.31), channel_id=1, source_target_pairs={{0,2},{1,6},{2,10},{3,14},{4,18},{5,22},{6,26},{7,30},{8,31},{9,27... | collective-permute-start | bytes 884744 | tf_op jit(solution)/shard_map/ppermute | solution.py:139
  69.7 4.5 %collective-permute-start.1 = (bf16[4,192,192]{2,1,0:T(8,128)(2,1)}, bf16[4,192,192]{2,1,0:T(8,128)(2,1)}, u32[]{:S(2)}, u32[]{:S(2)}) collective-permute-start(bf16[4,192,192]{2,1,0:T(8,128)(2,1)} %get-tuple-element.28), channel_id=1, source_target_pairs={{0,0},{1,4},{2,8},{3,12},{4,16},{5,20},{6,24},{7,28},{8,29},{9,25}... | collective-permute-start | bytes 884744 | tf_op jit(solution)/shard_map/ppermute | solution.py:139
  76.4 16.5 %fusion.217 = (f32[12,128]{1,0:T(8,128)S(1)}, f32[12,128,256]{2,1,0:T(8,128)}) fusion(f32[256]{0:T(256)S(1)} %bitcast.280, bf16[24,134,256]{2,1,0:T(8,128)(2,1)S(1)} %get-tuple-element.25, f32[256]{0:T(256)S(1)} %bitcast.281, f32[256]{0:T(256)S(1)} %bitcast.282, f32[256]{0:T(256)S(1)} %bitcast.283, bf16[6,128,256]{2,1,0:T(8,128)(2,1)S(1)} %collective-permute-done.6, ...), kind=kLoop, calls=%fused_computation.385 | loop fusion | flops 60160512 | bytes 36232192 | tf_op jit(solution)/shard_map/reduce_sum | solution.py:32
  96.3 2.2 fusion.97
  100.6 5.9 %all-to-all-start.2 = ((bf16[6,256,384]{2,0,1:T(8,128)(2,1)}), bf16[6,256,384]{2,0,1:T(8,128)(2,1)}, u32[]{:S(2)}, u32[]{:S(2)}) async-start(bf16[6,256,384]{2,0,1:T(8,128)(2,1)} %copy.76), calls=%async_computation.2 | async-start | bytes 3145728 | tf_op jit(solution)/shard_map/all_to_all | solution.py:161
  106.6 4.2 %fusion.63 = bf16[12,128,256]{2,1,0:T(8,128)(2,1)S(1)} fusion(bf16[12,128,256]{2,1,0:T(8,128)(2,1)S(1)} %add_convert_fusion.1, f32[12,128,256]{2,1,0:T(8,128)} %get-tuple-element.7, f32[256]{0:T(256)S(1)} %bitcast.329, f32[12,128]{1,0:T(8,128)S(1)} %add_rsqrt_fusion.3, f32[12,128]{1,0:T(8,128)S(1)} %broadcast_multiply_fusion.3, ...), kind=kOutput, calls=%fused_computation.78 | convolution fusion | flops 1627521024 | bytes 4207616 | tf_op jit(solution)/shard_map/dot_general | solution.py:235
  112.2 3.1 %collective-permute-start.9 = (bf16[6,128,256]{2,1,0:T(8,128)(2,1)S(1)}, bf16[6,128,256]{2,1,0:T(8,128)(2,1)S(1)}, u32[]{:S(2)}, u32[]{:S(2)}) collective-permute-start(bf16[6,128,256]{2,1,0:T(8,128)(2,1)S(1)} %get-tuple-element.32), channel_id=1, source_target_pairs={{0,1},{1,4},{4,5},{5,8},{8,9},{9,12},{12,13},{13,16},{16,17},{17,2... | collective-permute-start | bytes 1179656 | tf_op jit(solution)/shard_map/ppermute | solution.py:23
  115.3 2.5 add_select_fusion.1
  117.8 11.2 %collective-permute-start.11 = (bf16[24,6,256]{2,1,0:T(8,128)(2,1)S(1)}, bf16[24,6,256]{2,1,0:T(8,128)(2,1)S(1)}, u32[]{:S(2)}, u32[]{:S(2)}) collective-permute-start(bf16[24,6,256]{2,1,0:T(8,128)(2,1)S(1)} %get-tuple-element.22), channel_id=1, source_target_pairs={{0,2},{1,3},{4,6},{5,7},{8,10},{9,11},{12,14},{13,15},{16,18},{17,... | collective-permute-start | bytes 221192 | tf_op jit(solution)/shard_map/ppermute | solution.py:23
  132.3 3.2 %collective-permute-done.12 = bf16[24,6,256]{2,1,0:T(8,128)(2,1)S(1)} collective-permute-done((bf16[24,6,256]{2,1,0:T(8,128)(2,1)S(1)}, bf16[24,6,256]{2,1,0:T(8,128)(2,1)S(1)}, u32[]{:S(2)}, u32[]{:S(2)}) %collective-permute-start.12) | collective-permute-done | bytes 73760 | tf_op jit(solution)/shard_map/ppermute | solution.py:26
  137.3 21.9 %all-to-all-done.2 = bf16[6,256,384]{2,0,1:T(8,128)(2,1)} async-done(((bf16[6,256,384]{2,0,1:T(8,128)(2,1)}), bf16[6,256,384]{2,0,1:T(8,128)(2,1)}, u32[]{:S(2)}, u32[]{:S(2)}) %all-to-all-start.2) | async-done | bytes 1179680 | tf_op jit(solution)/shard_map/all_to_all | solution.py:161
  159.2 2.8 %copy.97 = bf16[32,6,8,384]{3,1,0,2:T(8,128)(2,1)} copy(bf16[32,6,8,384]{3,1,2,0:T(8,128)(2,1)} %bitcast.13) | data formatting | bytes 2359296 | tf_op jit(solution)/shard_map/reshape | solution.py:164
  162.0 3.3 %reshape.223 = bf16[192,4,2,384]{3,0,2,1:T(8,128)(2,1)} reshape(bf16[32,6,8,384]{3,1,0,2:T(8,128)(2,1)} %copy.97) | data formatting | bytes 2359296 | tf_op jit(solution)/shard_map/reshape | solution.py:164
  165.3 2.8 %convolution_convert_fusion = bf16[4,2,192,768]{3,2,1,0:T(8,128)(2,1)S(1)} fusion(bf16[192,4,2,384]{3,0,2,1:T(8,128)(2,1)} %reshape.223, bf16[384,384]{1,0:T(8,128)(2,1)} %param.25, bf16[384,384]{1,0:T(8,128)(2,1)} %param.24), kind=kOutput, calls=%fused_computation.44 | convolution fusion | flops 908328960 | bytes 4128768 | tf_op jit(solution)/shard_map/dot_general | solution.py:165
  173.6 19.7 %all-to-all-start.3 = ((bf16[192,8,384]{2,1,0:T(8,128)(2,1)}), bf16[192,8,384]{2,1,0:T(8,128)(2,1)}, u32[]{:S(2)}, u32[]{:S(2)}) async-start(bf16[192,8,384]{2,1,0:T(8,128)(2,1)} %copy.83), calls=%async_computation.3 | async-start | bytes 2359296 | tf_op jit(solution)/shard_map/all_to_all | solution.py:172
  193.4 22.6 %fusion.215 = (f32[12,128]{1,0:T(8,128)S(1)}, f32[12,128,256]{2,1,0:T(8,128)S(1)}) fusion(f32[256]{0:T(256)S(1)} %bitcast.231, bf16[24,134,256]{2,1,0:T(8,128)(2,1)} %get-tuple-element.21, f32[256]{0:T(256)S(1)} %bitcast.232, f32[256]{0:T(256)S(1)} %bitcast.233, f32[256]{0:T(256)S(1)} %bitcast.234, bf16[6,128,256]{2,1,0:T(8,128)(2,1)S(1)} %collective-permute-done.10, ...), kind=kLoop, calls=%fused_computation.384 | loop fusion | flops 60160512 | bytes 36232192 | tf_op jit(solution)/shard_map/reduce_sum | solution.py:32
  217.8 4.5 %all-to-all-done.3 = bf16[192,8,384]{2,1,0:T(8,128)(2,1)} async-done(((bf16[192,8,384]{2,1,0:T(8,128)(2,1)}), bf16[192,8,384]{2,1,0:T(8,128)(2,1)}, u32[]{:S(2)}, u32[]{:S(2)}) %all-to-all-start.3) | async-done | bytes 1179680 | tf_op jit(solution)/shard_map/all_to_all | solution.py:172
  222.3 2.8 %fusion.98 = bf16[6,256,384]{1,2,0:T(8,128)(2,1)S(1)} fusion(bf16[6,32,8,384]{3,2,0,1:T(8,128)(2,1)} %bitcast.26, s32[256]{0:T(256)S(1)} %copy-done.74, pred[256]{0:T(512)(128)(4,1)S(1)} %copy-done.76), kind=kOutput, calls=%fused_computation.123 | convolution fusion | flops 303759360 | bytes 2360576 | tf_op jit(solution)/shard_map/rn,trc->tnc/dot_general | solution.py:173
  225.2 2.1 copy.86
  227.2 4.8 %all-to-all-start.4 = ((bf16[6,256,384]{2,0,1:T(8,128)(2,1)}), bf16[6,256,384]{2,0,1:T(8,128)(2,1)}, u32[]{:S(2)}, u32[]{:S(2)}) async-start(bf16[6,256,384]{2,0,1:T(8,128)(2,1)} %copy.86), calls=%async_computation.4 | async-start | bytes 3145728 | tf_op jit(solution)/shard_map/all_to_all | solution.py:176
  232.1 5.0 %fusion.119 = bf16[12,128,256]{2,1,0:T(8,128)(2,1)} fusion(bf16[12,128,256]{2,1,0:T(8,128)(2,1)} %param.20, bf16[12,128,256]{2,1,0:T(8,128)(2,1)S(1)} %fusion.63, f32[12,128,256]{2,1,0:T(8,128)S(1)} %copy-done.4, f32[256]{0:T(256)S(1)} %bitcast.328, f32[12,128]{1,0:T(8,128)S(1)} %add_rsqrt_fusion.2, f32[12,128]{1,0:T(8,128)S(1)} %broadcast_multiply_fusion.2, ...), kind=kOutput, calls=%fused_computation.158 | convolution fusion | flops 1627914240 | bytes 4995584 | tf_op jit(solution)/shard_map/dot_general | solution.py:235
  237.0 14.8 %all-to-all-done.4 = bf16[6,256,384]{2,0,1:T(8,128)(2,1)} async-done(((bf16[6,256,384]{2,0,1:T(8,128)(2,1)}), bf16[6,256,384]{2,0,1:T(8,128)(2,1)}, u32[]{:S(2)}, u32[]{:S(2)}) %all-to-all-start.4) | async-done | bytes 1179680 | tf_op jit(solution)/shard_map/all_to_all | solution.py:176
  256.3 5.1 %add_convert_fusion = bf16[24,64,384]{2,1,0:T(8,128)(2,1)} fusion(f32[24,64,384]{2,1,0:T(8,128)S(1)} %get-tuple-element.9, f32[384]{0:T(512)S(1)} %copy-done.68, f32[24,64]{1,0:T(8,128)S(1)} %add_rsqrt_fusion, f32[24,64]{1,0:T(8,128)S(1)} %broadcast_multiply_fusion, bf16[768,384]{1,0:T(8,128)(2,1)S(1)} %copy-done, bf16[384,768]{1,0:T(8,128)(2,1)} %param.28), kind=kOutput, calls=%fused_computation.35 | convolution fusion | flops 1826095104 | bytes 4732416 | tf_op jit(solution)/shard_map/dot_general | solution.py:289
  (239 shorter events, 55.7 us)
Async XLA Ops:
  0.6 255.6 %copy-start = (bf16[768,384]{1,0:T(8,128)(2,1)S(1)}, bf16[768,384]{1,0:T(8,128)(2,1)}, u32[]{:S(2)}) copy-start(bf16[768,384]{1,0:T(8,128)(2,1)} %param.29) | copy-start | bytes 1769476
  4.4 10.0 %all-to-all-start = ((bf16[2,2,12288]{2,1,0:T(2,128)(2,1)}), bf16[2,2,12288]{2,1,0:T(2,128)(2,1)S(1)}, u32[]{:S(2)}, u32[]{:S(2)}) async-start(bf16[2,2,12288]{2,1,0:T(2,128)(2,1)} %reshape.226), calls=%async_computation | async-start | bytes 196608 | tf_op jit(solution)/shard_map/all_to_all | solution.py:270
  11.4 36.1 %collective-permute-start = (bf16[1,192,192]{2,1,0:T(8,128)(2,1)S(1)}, bf16[1,192,192]{2,1,0:T(8,128)(2,1)}, u32[]{:S(2)}, u32[]{:S(2)}) collective-permute-start(bf16[1,192,192]{2,1,0:T(8,128)(2,1)S(1)} %slice.968), channel_id=1, source_target_pairs={{9,8},{10,9},{11,10},{12,11},{13,12},{14,13},{15,14},{8,15},{25,24... | collective-permute-start | bytes 221192 | tf_op jit(solution)/shard_map/ppermute | solution.py:128
  14.4 9.4 %all-to-all-start.5 = ((bf16[2,2,12288]{2,1,0:T(2,128)(2,1)}), bf16[2,2,12288]{2,1,0:T(2,128)(2,1)S(1)}, u32[]{:S(2)}, u32[]{:S(2)}) async-start(bf16[2,2,12288]{2,1,0:T(2,128)(2,1)} %reshape.228), calls=%async_computation.5 | async-start | bytes 196608 | tf_op jit(solution)/shard_map/all_to_all | solution.py:271
  23.8 71.1 %all-to-all-start.1 = ((bf16[24,64,384]{2,1,0:T(8,128)(2,1)}), bf16[24,64,384]{2,1,0:T(8,128)(2,1)}, u32[]{:S(2)}, u32[]{:S(2)}) async-start(bf16[24,64,384]{2,1,0:T(8,128)(2,1)} %multiply_convert_fusion.4), calls=%async_computation.1 | async-start | bytes 2359296 | tf_op jit(solution)/shard_map/all_to_all | solution.py:157
  31.4 17.8 %collective-permute-start.6 = (bf16[6,128,256]{2,1,0:T(8,128)(2,1)}, bf16[6,128,256]{2,1,0:T(8,128)(2,1)S(1)}, u32[]{:S(2)}, u32[]{:S(2)}) collective-permute-start(bf16[6,128,256]{2,1,0:T(8,128)(2,1)} %get-tuple-element.35), channel_id=1, source_target_pairs={{1,0},{4,1},{5,4},{8,5},{9,8},{12,9},{13,12},{16,13},{17,16},{20,1... | collective-permute-start | bytes 1179656 | tf_op jit(solution)/shard_map/ppermute | solution.py:26
  32.8 16.3 %collective-permute-start.5 = (bf16[6,128,256]{2,1,0:T(8,128)(2,1)}, bf16[6,128,256]{2,1,0:T(8,128)(2,1)}, u32[]{:S(2)}, u32[]{:S(2)}) collective-permute-start(bf16[6,128,256]{2,1,0:T(8,128)(2,1)} %get-tuple-element.34), channel_id=1, source_target_pairs={{0,1},{1,4},{4,5},{5,8},{8,9},{9,12},{12,13},{13,16},{16,17},{17,2... | collective-permute-start | bytes 1179656 | tf_op jit(solution)/shard_map/ppermute | solution.py:23
  50.0 19.3 %collective-permute-start.7 = (bf16[24,6,256]{2,1,0:T(8,128)(2,1)S(1)}, bf16[24,6,256]{2,1,0:T(8,128)(2,1)S(1)}, u32[]{:S(2)}, u32[]{:S(2)}) collective-permute-start(bf16[24,6,256]{2,1,0:T(8,128)(2,1)S(1)} %get-tuple-element.26), channel_id=1, source_target_pairs={{0,2},{1,3},{4,6},{5,7},{8,10},{9,11},{12,14},{13,15},{16,18},{17,... | collective-permute-start | bytes 221192 | tf_op jit(solution)/shard_map/ppermute | solution.py:23
  54.8 19.4 %collective-permute-start.8 = (bf16[24,6,256]{2,1,0:T(8,128)(2,1)S(1)}, bf16[24,6,256]{2,1,0:T(8,128)(2,1)S(1)}, u32[]{:S(2)}, u32[]{:S(2)}) collective-permute-start(bf16[24,6,256]{2,1,0:T(8,128)(2,1)S(1)} %get-tuple-element.27), channel_id=1, source_target_pairs={{2,0},{3,1},{6,4},{7,5},{10,8},{11,9},{14,12},{15,13},{18,16},{19,... | collective-permute-start | bytes 221192 | tf_op jit(solution)/shard_map/ppermute | solution.py:26
  57.2 54.9 %collective-permute-start.4 = (bf16[4,192,192]{2,1,0:T(8,128)(2,1)}, bf16[4,192,192]{2,1,0:T(8,128)(2,1)}, u32[]{:S(2)}, u32[]{:S(2)}) collective-permute-start(bf16[4,192,192]{2,1,0:T(8,128)(2,1)} %get-tuple-element.29), channel_id=1, source_target_pairs={{0,3},{1,7},{2,11},{3,15},{4,19},{5,23},{6,27},{7,31},{8,28},{9,24... | collective-permute-start | bytes 884744 | tf_op jit(solution)/shard_map/ppermute | solution.py:139
  61.8 53.5 %collective-permute-start.3 = (bf16[4,192,192]{2,1,0:T(8,128)(2,1)}, bf16[4,192,192]{2,1,0:T(8,128)(2,1)}, u32[]{:S(2)}, u32[]{:S(2)}) collective-permute-start(bf16[4,192,192]{2,1,0:T(8,128)(2,1)} %get-tuple-element.30), channel_id=1, source_target_pairs={{0,1},{1,5},{2,9},{3,13},{4,17},{5,21},{6,25},{7,29},{8,30},{9,26}... | collective-permute-start | bytes 884744 | tf_op jit(solution)/shard_map/ppermute | solution.py:139
  65.9 49.3 %collective-permute-start.2 = (bf16[4,192,192]{2,1,0:T(8,128)(2,1)}, bf16[4,192,192]{2,1,0:T(8,128)(2,1)}, u32[]{:S(2)}, u32[]{:S(2)}) collective-permute-start(bf16[4,192,192]{2,1,0:T(8,128)(2,1)} %get-tuple-element.31), channel_id=1, source_target_pairs={{0,2},{1,6},{2,10},{3,14},{4,18},{5,22},{6,26},{7,30},{8,31},{9,27... | collective-permute-start | bytes 884744 | tf_op jit(solution)/shard_map/ppermute | solution.py:139
  69.7 45.6 %collective-permute-start.1 = (bf16[4,192,192]{2,1,0:T(8,128)(2,1)}, bf16[4,192,192]{2,1,0:T(8,128)(2,1)}, u32[]{:S(2)}, u32[]{:S(2)}) collective-permute-start(bf16[4,192,192]{2,1,0:T(8,128)(2,1)} %get-tuple-element.28), channel_id=1, source_target_pairs={{0,0},{1,4},{2,8},{3,12},{4,16},{5,20},{6,24},{7,28},{8,29},{9,25}... | collective-permute-start | bytes 884744 | tf_op jit(solution)/shard_map/ppermute | solution.py:139
  100.6 58.7 %all-to-all-start.2 = ((bf16[6,256,384]{2,0,1:T(8,128)(2,1)}), bf16[6,256,384]{2,0,1:T(8,128)(2,1)}, u32[]{:S(2)}, u32[]{:S(2)}) async-start(bf16[6,256,384]{2,0,1:T(8,128)(2,1)} %copy.76), calls=%async_computation.2 | async-start | bytes 3145728 | tf_op jit(solution)/shard_map/all_to_all | solution.py:161
  110.9 6.9 %collective-permute-start.10 = (bf16[6,128,256]{2,1,0:T(8,128)(2,1)S(1)}, bf16[6,128,256]{2,1,0:T(8,128)(2,1)S(1)}, u32[]{:S(2)}, u32[]{:S(2)}) collective-permute-start(bf16[6,128,256]{2,1,0:T(8,128)(2,1)S(1)} %get-tuple-element.33), channel_id=1, source_target_pairs={{1,0},{4,1},{5,4},{8,5},{9,8},{12,9},{13,12},{16,13},{17,16},{20,1... | collective-permute-start | bytes 1179656 | tf_op jit(solution)/shard_map/ppermute | solution.py:26
  112.2 5.6 %collective-permute-start.9 = (bf16[6,128,256]{2,1,0:T(8,128)(2,1)S(1)}, bf16[6,128,256]{2,1,0:T(8,128)(2,1)S(1)}, u32[]{:S(2)}, u32[]{:S(2)}) collective-permute-start(bf16[6,128,256]{2,1,0:T(8,128)(2,1)S(1)} %get-tuple-element.32), channel_id=1, source_target_pairs={{0,1},{1,4},{4,5},{5,8},{8,9},{9,12},{12,13},{13,16},{16,17},{17,2... | collective-permute-start | bytes 1179656 | tf_op jit(solution)/shard_map/ppermute | solution.py:23
  117.8 14.5 %collective-permute-start.11 = (bf16[24,6,256]{2,1,0:T(8,128)(2,1)S(1)}, bf16[24,6,256]{2,1,0:T(8,128)(2,1)S(1)}, u32[]{:S(2)}, u32[]{:S(2)}) collective-permute-start(bf16[24,6,256]{2,1,0:T(8,128)(2,1)S(1)} %get-tuple-element.22), channel_id=1, source_target_pairs={{0,2},{1,3},{4,6},{5,7},{8,10},{9,11},{12,14},{13,15},{16,18},{17,... | collective-permute-start | bytes 221192 | tf_op jit(solution)/shard_map/ppermute | solution.py:23
  129.0 6.5 %collective-permute-start.12 = (bf16[24,6,256]{2,1,0:T(8,128)(2,1)S(1)}, bf16[24,6,256]{2,1,0:T(8,128)(2,1)S(1)}, u32[]{:S(2)}, u32[]{:S(2)}) collective-permute-start(bf16[24,6,256]{2,1,0:T(8,128)(2,1)S(1)} %get-tuple-element.23), channel_id=1, source_target_pairs={{2,0},{3,1},{6,4},{7,5},{10,8},{11,9},{14,12},{15,13},{18,16},{19,... | collective-permute-start | bytes 221192 | tf_op jit(solution)/shard_map/ppermute | solution.py:26
  173.5 19.9 %copy-start.19 = (f32[1,1,256]{2,1,0:T(1,128)S(1)}, f32[1,1,256]{2,1,0:T(1,128)}, u32[]{:S(2)}) copy-start(f32[1,1,256]{2,1,0:T(1,128)} %get-tuple-element.54) | copy-start | bytes 3076
  173.5 19.9 %copy-start.20 = (f32[1,1,256]{2,1,0:T(1,128)S(1)}, f32[1,1,256]{2,1,0:T(1,128)}, u32[]{:S(2)}) copy-start(f32[1,1,256]{2,1,0:T(1,128)} %get-tuple-element.55) | copy-start | bytes 3076
  173.5 19.9 %copy-start.21 = (f32[1,1,256]{2,1,0:T(1,128)S(1)}, f32[1,1,256]{2,1,0:T(1,128)}, u32[]{:S(2)}) copy-start(f32[1,1,256]{2,1,0:T(1,128)} %get-tuple-element.56) | copy-start | bytes 3076
  173.5 19.9 %copy-start.22 = (f32[1,1,256]{2,1,0:T(1,128)S(1)}, f32[1,1,256]{2,1,0:T(1,128)}, u32[]{:S(2)}) copy-start(f32[1,1,256]{2,1,0:T(1,128)} %get-tuple-element.57) | copy-start | bytes 3076
  173.5 19.9 %copy-start.23 = (f32[1,1,256]{2,1,0:T(1,128)S(1)}, f32[1,1,256]{2,1,0:T(1,128)}, u32[]{:S(2)}) copy-start(f32[1,1,256]{2,1,0:T(1,128)} %get-tuple-element.58) | copy-start | bytes 3076
  173.5 19.9 %copy-start.24 = (f32[1,1,256]{2,1,0:T(1,128)S(1)}, f32[1,1,256]{2,1,0:T(1,128)}, u32[]{:S(2)}) copy-start(f32[1,1,256]{2,1,0:T(1,128)} %get-tuple-element.59) | copy-start | bytes 3076
  173.5 19.9 %copy-start.25 = (f32[1,1,256]{2,1,0:T(1,128)S(1)}, f32[1,1,256]{2,1,0:T(1,128)}, u32[]{:S(2)}) copy-start(f32[1,1,256]{2,1,0:T(1,128)} %get-tuple-element.60) | copy-start | bytes 3076
  173.5 19.9 %copy-start.26 = (f32[1,1,256]{2,1,0:T(1,128)S(1)}, f32[1,1,256]{2,1,0:T(1,128)}, u32[]{:S(2)}) copy-start(f32[1,1,256]{2,1,0:T(1,128)} %get-tuple-element.61) | copy-start | bytes 3076
  173.5 19.9 %copy-start.27 = (f32[1,1,256]{2,1,0:T(1,128)S(1)}, f32[1,1,256]{2,1,0:T(1,128)}, u32[]{:S(2)}) copy-start(f32[1,1,256]{2,1,0:T(1,128)} %get-tuple-element.62) | copy-start | bytes 3076
  173.5 19.9 %copy-start.28 = (f32[1,1,256]{2,1,0:T(1,128)S(1)}, f32[1,1,256]{2,1,0:T(1,128)}, u32[]{:S(2)}) copy-start(f32[1,1,256]{2,1,0:T(1,128)} %get-tuple-element.63) | copy-start | bytes 3076
  173.5 19.9 %copy-start.29 = (f32[1,1,256]{2,1,0:T(1,128)S(1)}, f32[1,1,256]{2,1,0:T(1,128)}, u32[]{:S(2)}) copy-start(f32[1,1,256]{2,1,0:T(1,128)} %get-tuple-element.64) | copy-start | bytes 3076
  173.6 19.9 %copy-start.30 = (f32[1,1,256]{2,1,0:T(1,128)S(1)}, f32[1,1,256]{2,1,0:T(1,128)}, u32[]{:S(2)}) copy-start(f32[1,1,256]{2,1,0:T(1,128)} %get-tuple-element.65) | copy-start | bytes 3076
  173.6 48.7 %all-to-all-start.3 = ((bf16[192,8,384]{2,1,0:T(8,128)(2,1)}), bf16[192,8,384]{2,1,0:T(8,128)(2,1)}, u32[]{:S(2)}, u32[]{:S(2)}) async-start(bf16[192,8,384]{2,1,0:T(8,128)(2,1)} %copy.83), calls=%async_computation.3 | async-start | bytes 2359296 | tf_op jit(solution)/shard_map/all_to_all | solution.py:172
  227.2 24.6 %all-to-all-start.4 = ((bf16[6,256,384]{2,0,1:T(8,128)(2,1)}), bf16[6,256,384]{2,0,1:T(8,128)(2,1)}, u32[]{:S(2)}, u32[]{:S(2)}) async-start(bf16[6,256,384]{2,0,1:T(8,128)(2,1)} %copy.86), calls=%async_computation.4 | async-start | bytes 3145728 | tf_op jit(solution)/shard_map/all_to_all | solution.py:176
  (64 other events, 415.3 us)

commit v2 on v1

--- a/solution.py
+++ b/solution.py
@@ -3,6 +3,8 @@
 import jax
 import jax.numpy as jnp
 from jax import lax
+from jax.experimental import pallas as pl
+from jax.experimental.pallas import tpu as pltpu
 from jax.sharding import PartitionSpec as P
 
 MODES = 512
@@ -44,7 +46,7 @@
 
 
 def forward_table(row_index, circle):
-    wavenumber, waves = wave_table(row_index, circle)
+    _, waves = wave_table(row_index, circle)
     return (waves.T / math.sqrt(circle)).astype(jnp.bfloat16)
 
 
@@ -98,9 +100,19 @@
     )
 
 
-def folded_waves(circle):
+def place_of(kind, i, group):
+    return kind * group + (group - 1 - i if kind % 2 else i)
+
+
+def folded_waves(circle, devices):
     longitude = jnp.arange(circle, dtype=jnp.int32)
-    row_index = jnp.arange(circle, dtype=jnp.int32)
+    position = jnp.arange(circle, dtype=jnp.int32)
+    group = devices // 4
+    owned = circle // devices
+    owner = position // owned
+    kind, place = owner // group, owner % group
+    place = jnp.where(kind % 2 == 1, group - 1 - place, place)
+    row_index = (4 * place + kind) * owned + position % owned
     wavenumber = jnp.where(row_index == 1, circle // 2, row_index // 2)
     phases = wavenumber[:, None] * longitude[None, :] % circle
     angles = phases.astype(jnp.float32) * (2.0 * math.pi / circle)
@@ -111,12 +123,14 @@
 def folded_operators(table, quad_weight, degree_gain):
     devices = lax.axis_size(EVERY)
     me = lax.axis_index(EVERY)
-    count, degrees, lat_total = table.shape
+    count, _, lat_total = table.shape
     group = devices // 4
     part = count // 4
     family = me // group
     scaled = (table.astype(jnp.float32) * degree_gain[:, None]).astype(jnp.bfloat16)
-    operators = jnp.einsum("mlt,mlu->mtu", table, scaled, preferred_element_type=jnp.float32)
+    operators = jnp.einsum(
+        "mlt,mlu->mtu", table, scaled, preferred_element_type=jnp.float32
+    )
     operators = operators * (quad_weight / lat_total)
     first_scale = jnp.where(me == 0, 0.5, 1.0).astype(jnp.float32)
     scales = jnp.where(jnp.arange(count) == 0, first_scale, 1.0)
@@ -128,19 +142,19 @@
     rotated = lax.ppermute(operators[:1], EVERY, turn)
     mirrored = jnp.concatenate([rotated, jnp.flip(operators[1:], axis=0)], axis=0)
     ordered = jnp.where(family % 2 == 1, mirrored, operators)
-    received = []
-    for step in range(4):
+    received = [lax.dynamic_slice_in_dim(ordered, family * part, part, axis=0)]
+    for shift in range(1, 4):
         pairs = []
-        for source in range(devices):
-            kind, place = source // group, source % group
-            place = group - 1 - place if kind % 2 else place
-            pairs.append((source, 4 * place + (step + kind) % 4))
-        piece = lax.dynamic_slice_in_dim(ordered, (step + family) % 4 * part, part, axis=0)
-        received.append(lax.ppermute(piece, EVERY, pairs).astype(jnp.float32))
-    even = received[0] + received[2]
-    odd = received[1] + received[3]
-    direct = jnp.where(me % 2 == 0, even, odd)
-    mirror = jnp.where(me % 2 == 0, odd, even)
+        for i in range(group):
+            for kind in range(4):
+                pairs.append((place_of(kind, i, group), place_of(kind ^ shift, i, group)))
+        piece = lax.dynamic_slice_in_dim(ordered, (family ^ shift) * part, part, axis=0)
+        received.append(lax.ppermute(piece, EVERY, pairs))
+    received = [value.astype(jnp.float32) for value in received]
+    same = received[0] + received[2]
+    other = received[1] + received[3]
+    direct = jnp.where(family % 2 == 0, same, other)
+    mirror = jnp.where(family % 2 == 0, other, same)
     lone = ((me == 0) & (jnp.arange(part) == 0))[:, None, None]
     both = direct + mirror
     gap = jnp.where(lone, 0.0, direct - mirror)
@@ -153,7 +167,7 @@
     width = normed.shape[2]
     top, bottom = folded_operators(legendre, quad_weight, degree_gain)
     slots = top.shape[0]
-    waves = folded_waves(circle).astype(jnp.bfloat16)
+    waves = folded_waves(circle, lax.axis_size(EVERY)).astype(jnp.bfloat16)
     columns = lax.all_to_all(normed, COLUMNS, split_axis=0, concat_axis=1, tiled=True)
     spectrum = jnp.einsum(
         "rn,tnc->trc", waves, columns, preferred_element_type=jnp.float32
@@ -173,7 +187,8 @@
     spatial = jnp.einsum(
         "rn,trc->tnc", waves, returned, preferred_element_type=jnp.float32
     ).astype(jnp.bfloat16)
-    return lax.all_to_all(spatial, COLUMNS, split_axis=1, concat_axis=0, tiled=True)
+    spectral = lax.all_to_all(spatial, COLUMNS, split_axis=1, concat_axis=0, tiled=True)
+    return spectral, (spectrum, filtered)
 
 
 def plain_spectral(normed, legendre, quad_weight, spec_real, spec_imag, degree_gain, circle):
@@ -206,7 +221,8 @@
     spatial = jnp.einsum(
         "arc,rn->anc", returned, inverse, preferred_element_type=jnp.float32
     ).astype(jnp.bfloat16)
-    return lax.all_to_all(spatial, ("lon", "comp"), split_axis=1, concat_axis=2, tiled=True)
+    spectral = lax.all_to_all(spatial, COLUMNS, split_axis=1, concat_axis=2, tiled=True)
+    return spectral, (spectrum, filtered)
 
 
 def ocean_block(padded_field, kernel, gain, up_weight, down_weight):
@@ -234,6 +250,73 @@
         centre.astype(jnp.float32)
         + jnp.dot(hidden, down_weight, preferred_element_type=jnp.float32)
     ).astype(jnp.bfloat16)
+
+
+def ocean_kernel_body(
+    field_ref, taps_ref, gain_ref, up_ref, down_ref, after_ref, out_ref, wide, normed
+):
+    rows, cols, width = out_ref.shape
+    step = OCEAN_DILATION
+    lanes = 128
+
+    @pl.loop(0, rows + (STENCIL_TAPS - 1) * step)
+    def _(row):
+        wide[row] = field_ref[row].astype(jnp.float32)
+
+    @pl.loop(0, rows // 2)
+    def _(pair):
+        base = pair // step * (2 * step) + pair % step
+        for half in range(width // lanes):
+            part = slice(half * lanes, (half + 1) * lanes)
+            sums = [jnp.zeros((cols, lanes), jnp.float32) for _ in range(2)]
+            for a in range(STENCIL_TAPS + 1):
+                for b in range(STENCIL_TAPS):
+                    window = wide[base + a * step, b * step : b * step + cols, part]
+                    for which in range(2):
+                        tap = a - which
+                        if 0 <= tap < STENCIL_TAPS:
+                            weight = taps_ref[tap * STENCIL_TAPS + b, :, part]
+                            sums[which] = sums[which] + window * weight
+            for which in range(2):
+                normed[which * cols : (which + 1) * cols, part] = sums[which]
+        stencil = normed[...]
+        values = layer_norm(stencil, gain_ref[...]).astype(jnp.bfloat16)
+        hidden = jax.nn.gelu(
+            jnp.dot(values, up_ref[...], preferred_element_type=jnp.float32)
+        ).astype(jnp.bfloat16)
+        moved = jnp.dot(hidden, down_ref[...], preferred_element_type=jnp.float32)
+        reach = STENCIL_TAPS // 2 * step
+        for which in range(2):
+            row = base + which * step
+            centre = wide[row + reach, reach : reach + cols, :]
+            out_ref[row] = (centre + moved[which * cols : (which + 1) * cols]).astype(
+                out_ref.dtype
+            )
+
+
+def fast_ocean_block(field, kernel, gain, up_weight, down_weight, after):
+    reach = STENCIL_TAPS // 2 * OCEAN_DILATION
+    rows, cols, width = field.shape[0] - 2 * reach, field.shape[1] - 2 * reach, field.shape[2]
+    hidden = up_weight.shape[1]
+    taps = kernel.astype(jnp.float32).reshape(STENCIL_TAPS * STENCIL_TAPS, 1, width)
+    whole = pl.BlockSpec(memory_space=pltpu.VMEM)
+    cells = rows * cols
+    return pl.pallas_call(
+        ocean_kernel_body,
+        out_shape=jax.ShapeDtypeStruct((rows, cols, width), jnp.bfloat16),
+        in_specs=[whole] * 5 + [pl.BlockSpec(memory_space=pl.ANY)],
+        out_specs=whole,
+        scratch_shapes=[
+            pltpu.VMEM(field.shape, jnp.float32),
+            pltpu.VMEM((2 * cols, width), jnp.float32),
+        ],
+        compiler_params=pltpu.CompilerParams(vmem_limit_bytes=32 * 1024 * 1024),
+        cost_estimate=pl.CostEstimate(
+            flops=4 * cells * width * hidden + 98 * cells * width * 64,
+            bytes_accessed=4 * field.size + 4 * up_weight.size,
+            transcendentals=cells * hidden,
+        ),
+    )(field, taps, gain[None, :], up_weight, down_weight, after)
 
 
 def local(
@@ -258,7 +341,7 @@
     ocean_down,
 ):
     col_count = lax.axis_size(COLUMNS)
-    lat_dev, lon_dev, width = atm_state.shape
+    lat_dev, lon_dev, _ = atm_state.shape
     circle = lon_dev * col_count
     wet = wet_mask.astype(jnp.float32)[:, :, None]
     ocean_flux = (
@@ -278,7 +361,7 @@
         if folds(circle, lat_dev, col_count, lax.axis_size(EVERY))
         else plain_spectral
     )
-    spectral = run_spectral(
+    spectral, stages = run_spectral(
         normed, legendre, quad_weight, spec_real, spec_imag, degree_gain, circle
     )
     mixed = forced + spectral.astype(jnp.float32)
@@ -296,9 +379,14 @@
     stencil_reach = STENCIL_TAPS // 2 * OCEAN_DILATION
     sides = ((("lat", "comp"), 0), ("lon", 1))
     current = ocean_in
+    quick = ocean_in.shape[0] % (2 * OCEAN_DILATION) == 0 and ocean_in.shape[2] % 128 == 0
     for k in range(2):
         field = padded(current, sides, stencil_reach)
-        current = ocean_block(field, ocean_kernel[k], ocean_gain[k], ocean_up[k], ocean_down[k])
+        weights = (ocean_kernel[k], ocean_gain[k], ocean_up[k], ocean_down[k])
+        if quick:
+            current = fast_ocean_block(field, *weights, stages[k])
+        else:
+            current = ocean_block(field, *weights)
     ocean_out = jnp.where(wet_mask[:, :, None] == 1, current, ocean_state)
     return (atm_out, ocean_out)
 
@@ -325,6 +413,7 @@
         P(),
         P(),
     )
+
     return jax.shard_map(
         local,
         mesh=mesh,

time: 263 us -> 239 us (0.909)
  the two profiles are of different devices: /device:TPU:0 before, /device:TPU:20 now
where the time goes in v2:
time: 239 us; the launch traced here: 238 us
  waiting for transfers between devices  66.7 us (28%)
  starting transfers between devices  56.5 us (24%)
  local copies, waits for them, and re-layouts  39.9 us (17%)
  Pallas kernels  30.9 us (13%)
  matrix products  22.8 us (10%)
  other arithmetic  16 us (7%)
  blocking collectives  3.79 us (2%)
    ppermute x3, waiting for transfers between devices, folded_operators(): received.append(lax.ppermute(piece, EVERY, pairs))  36.6 us
    pallas_call x2, Pallas kernels, fast_ocean_block(): pl.pallas_call(ocean_kernel_body, out_shape=jax.ShapeDtypeStruct((rows, c...  30.9 us
    all_to_all x1, waiting for transfers between devices, folded_spectral(): lax.all_to_all(normed, COLUMNS, split_axis=0, concat_axis=1, tiled=True)  14 us
    ppermute x4, starting transfers between devices, padded(): lax.ppermute(lax.slice_in_dim(block, block.shape[dim] - width, None, axis...  13.8 us
    all_to_all x1, starting transfers between devices, folded_spectral(): lax.all_to_all(filtered, EVERY, split_axis=0, concat_axis=1, tiled=True)  11.5 us
    ppermute x4, waiting for transfers between devices, padded(): lax.ppermute(lax.slice_in_dim(block, 0, width, axis=dim), axis, backward)  10.2 us
    ppermute x4, starting transfers between devices, padded(): lax.ppermute(lax.slice_in_dim(block, 0, width, axis=dim), axis, backward)  6.94 us
    unnamed x48, local copies, waits for them, and re-layouts  6.35 us
  transfers between devices with their start and end apart: 17, of which 7 were waited for; matrix products, arithmetic and copies ran while one was open for 25% of the time, Pallas kernels for 13%

profile of v2, /device:TPU:20, one launch (start us, length us, event | category | flops | bytes accessed | tf_op | source)
XLA Modules:
  0.0 237.9 jit_solution(17726582569447069114)
XLA Ops:
  3.8 3.8 %all_to_all.96 = bf16[2,2,12288]{2,1,0:T(2,128)(2,1)S(1)} all-to-all(bf16[2,2,12288]{2,1,0:T(2,128)(2,1)S(1)} %reshape.193), channel_id=1, replica_groups=mesh['lat'=8,'lon'=2,'comp'=2] {'comp'}, dimensions={0} | all-to-all | bytes 196608 | tf_op jit(solution)/shard_map/all_to_all | solution.py:353
  12.0 3.7 %all-to-all-start.1 = ((bf16[24,64,384]{2,1,0:T(8,128)(2,1)}), bf16[24,64,384]{2,1,0:T(8,128)(2,1)S(1)}, u32[]{:S(2)}, u32[]{:S(2)}) async-start(bf16[24,64,384]{2,1,0:T(8,128)(2,1)} %multiply_convert_fusion.4), calls=%async_computation.1 | async-start | bytes 2359296 | tf_op jit(solution)/shard_map/all_to_all | solution.py:171
  17.4 14.0 %all-to-all-done.1 = bf16[24,64,384]{2,1,0:T(8,128)(2,1)S(1)} async-done(((bf16[24,64,384]{2,1,0:T(8,128)(2,1)}), bf16[24,64,384]{2,1,0:T(8,128)(2,1)S(1)}, u32[]{:S(2)}, u32[]{:S(2)}) %all-to-all-start.1) | async-done | bytes 1179680 | tf_op jit(solution)/shard_map/all_to_all | solution.py:171
  31.4 3.3 %all-to-all-start.5 = ((bf16[2,2,12288]{2,1,0:T(2,128)(2,1)}), bf16[2,2,12288]{2,1,0:T(2,128)(2,1)S(1)}, u32[]{:S(2)}, u32[]{:S(2)}) async-start(bf16[2,2,12288]{2,1,0:T(2,128)(2,1)} %reshape.195), calls=%async_computation.5 | async-start | bytes 196608 | tf_op jit(solution)/shard_map/all_to_all | solution.py:354
  38.7 5.1 %all-to-all-start.2 = ((bf16[6,256,384]{2,0,1:T(8,128)(2,1)}), bf16[6,256,384]{2,0,1:T(8,128)(2,1)}, u32[]{:S(2)}, u32[]{:S(2)}) async-start(bf16[6,256,384]{2,0,1:T(8,128)(2,1)} %copy.50), calls=%async_computation.2 | async-start | bytes 3145728 | tf_op jit(solution)/shard_map/all_to_all | solution.py:175
  43.8 4.6 %fusion.14 = bf16[16,192,192]{2,1,0:T(8,128)(2,1)} fusion(f32[16]{0:T(128)S(1)} %compare_select_fusion.3, f32[192]{0:T(256)S(1)} %broadcast_multiply_fusion.2, bf16[16,384,192]{1,2,0:T(8,128)(2,1)} %param.22, f32[384]{0:T(512)S(1)} %copy-done.21), kind=kOutput, calls=%fused_computation.29 | convolution fusion | flops 458293248 | bytes 3541312 | tf_op jit(solution)/shard_map/mlt,mlu->mtu/dot_general | solution.py:131
  55.4 2.3 collective-permute-start.4
  57.8 2.6 %slice.97 = bf16[15,192,192]{2,1,0:T(8,128)(2,1)} slice(bf16[16,192,192]{2,1,0:T(8,128)(2,1)} %fusion.14), slice={[1:16], [0:192], [0:192]} | slice | bytes 2211840 | tf_op jit(solution)/shard_map/slice | solution.py:143
  60.4 2.7 %rev.4 = bf16[15,192,192]{2,1,0:T(8,128)(2,1)} reverse(bf16[15,192,192]{2,1,0:T(8,128)(2,1)} %slice.97), dimensions={0} | reverse | bytes 2211840 | tf_op jit(solution)/shard_map/jit(_flip)/rev | solution.py:143
  67.5 2.9 %collective-permute-start.3 = (bf16[4,192,192]{2,1,0:T(8,128)(2,1)}, bf16[4,192,192]{2,1,0:T(8,128)(2,1)}, u32[]{:S(2)}, u32[]{:S(2)}) collective-permute-start(bf16[4,192,192]{2,1,0:T(8,128)(2,1)} %get-tuple-element.21), channel_id=1, source_target_pairs={{0,31},{15,16},{16,15},{31,0},{1,30},{14,17},{17,14},{30,1},{2,29}... | collective-permute-start | bytes 884744 | tf_op jit(solution)/shard_map/ppermute | solution.py:152
  71.4 2.4 collective-permute-start.1
  75.8 31.0 %collective-permute-done.3 = bf16[4,192,192]{2,1,0:T(8,128)(2,1)} collective-permute-done((bf16[4,192,192]{2,1,0:T(8,128)(2,1)}, bf16[4,192,192]{2,1,0:T(8,128)(2,1)}, u32[]{:S(2)}, u32[]{:S(2)}) %collective-permute-start.3) | collective-permute-done | bytes 294944 | tf_op jit(solution)/shard_map/ppermute | solution.py:152
  106.9 5.6 %collective-permute-done.1 = bf16[4,192,192]{2,1,0:T(8,128)(2,1)} collective-permute-done((bf16[4,192,192]{2,1,0:T(8,128)(2,1)}, bf16[4,192,192]{2,1,0:T(8,128)(2,1)}, u32[]{:S(2)}, u32[]{:S(2)}) %collective-permute-start.1) | collective-permute-done | bytes 294944 | tf_op jit(solution)/shard_map/ppermute | solution.py:152
  112.5 2.5 %add_select_fusion.1 = (f32[4,192,192]{2,1,0:T(8,128)}, f32[4,192,192]{2,1,0:T(8,128)S(1)}, f32[4,192,192]{2,1,0:T(8,128)S(1)}) fusion(pred[4]{0:T(512)(128)(4,1)S(1)} %compare_and_fusion, bf16[4,192,192]{2,1,0:T(8,128)(2,1)} %collective-permute-done.3, bf16[4,192,192]{2,1,0:T(8,128)(2,1)} %collective-permute-done.2, ...), kind=kLoop, calls=%fused_computation.59 | loop fusion | flops 1474560 | bytes 2949129 | tf_op jit(solution)/shard_map/jit(_where)/select_n | solution.py:161
  116.7 2.6 %copy.77 = bf16[6,32,8,384]{3,2,0,1:T(8,128)(2,1)} copy(bf16[6,32,8,384]{3,0,2,1:T(8,128)(2,1)} %bitcast.11) | data formatting | bytes 2359296 | tf_op jit(solution)/shard_map/all_to_all | solution.py:175
  119.3 3.6 %reshape.178 = bf16[192,4,2,384]{3,2,1,0:T(2,128)(2,1)} reshape(bf16[32,6,8,384]{3,2,1,0:T(8,128)(2,1)} %bitcast.118) | data formatting | bytes 2359296 | tf_op jit(solution)/shard_map/reshape | solution.py:178
  123.0 2.8 %convolution_convert_fusion = bf16[4,2,192,768]{3,2,1,0:T(8,128)(2,1)S(1)} fusion(bf16[192,4,2,384]{3,2,1,0:T(2,128)(2,1)} %reshape.178, bf16[384,384]{1,0:T(8,128)(2,1)} %param.25, bf16[384,384]{1,0:T(8,128)(2,1)} %param.24), kind=kOutput, calls=%fused_computation.22 | convolution fusion | flops 908328960 | bytes 4128768 | tf_op jit(solution)/shard_map/dot_general | solution.py:179
  128.5 2.2 copy.55
  130.8 3.8 %convert_element_type.146 = bf16[8,192,384]{2,0,1:T(8,128)(2,1)} reshape(bf16[4,2,192,384]{3,1,0,2:T(2,128)(2,1)} %copy.55) | data formatting | bytes 2359296 | tf_op jit(solution)/shard_map/convert_element_type | solution.py:184
  134.5 11.5 %all-to-all-start.3 = ((bf16[192,8,384]{2,1,0:T(8,128)(2,1)}), bf16[192,8,384]{2,1,0:T(8,128)(2,1)}, u32[]{:S(2)}, u32[]{:S(2)}) async-start(bf16[192,8,384]{2,1,0:T(8,128)(2,1)} %bitcast.22.after_ref), calls=%async_computation.3 | async-start | bytes 2359296 | tf_op jit(solution)/shard_map/all_to_all | solution.py:186
  150.4 4.8 %collective-permute-start.6 = (bf16[24,6,256]{2,1,0:T(8,128)(2,1)S(1)}, bf16[24,6,256]{2,1,0:T(8,128)(2,1)S(1)}, u32[]{:S(2)}, u32[]{:S(2)}) collective-permute-start(bf16[24,6,256]{2,1,0:T(8,128)(2,1)S(1)} %get-tuple-element.18), channel_id=1, source_target_pairs={{0,2},{1,3},{4,6},{5,7},{8,10},{9,11},{12,14},{13,15},{16,18},{17,... | collective-permute-start | bytes 221192 | tf_op jit(solution)/shard_map/ppermute | solution.py:25
  155.2 2.9 %collective-permute-done.7 = bf16[24,6,256]{2,1,0:T(8,128)(2,1)S(1)} collective-permute-done((bf16[24,6,256]{2,1,0:T(8,128)(2,1)S(1)}, bf16[24,6,256]{2,1,0:T(8,128)(2,1)S(1)}, u32[]{:S(2)}, u32[]{:S(2)}) %collective-permute-start.7) | collective-permute-done | bytes 73760 | tf_op jit(solution)/shard_map/ppermute | solution.py:28
  160.2 15.5 %shard_map.194 = bf16[12,128,256]{2,1,0:T(8,128)(2,1)S(1)} custom-call(bf16[24,140,256]{2,1,0:T(8,128)(2,1)S(1)} %pad_maximum_fusion.field_ref, f32[49,1,256]{2,1,0:T(1,128)S(1)} %bitcast_convert_fusion.1.taps_ref, f32[1,256]{1,0:T(1,128)S(1)} %get-tuple-element.34.gain_ref, bf16[256,1024]{1,0:T(8,128)(2,1)S(1)} %copy-done.1, ...), custom_call_target="tpu_custom_call" | custom-call | flops 4076863488 | bytes 4489216 | tf_op jit(solution)/shard_map/pallas_call | solution.py:304
  175.8 2.2 collective-permute-start.9
  180.2 7.3 %collective-permute-done.9 = bf16[6,128,256]{2,1,0:T(8,128)(2,1)S(1)} collective-permute-done((bf16[6,128,256]{2,1,0:T(8,128)(2,1)S(1)}, bf16[6,128,256]{2,1,0:T(8,128)(2,1)S(1)}, u32[]{:S(2)}, u32[]{:S(2)}) %collective-permute-start.9) | collective-permute-done | bytes 393248 | tf_op jit(solution)/shard_map/ppermute | solution.py:28
  187.5 3.8 %collective-permute-done.8 = bf16[6,128,256]{2,1,0:T(8,128)(2,1)S(1)} collective-permute-done((bf16[6,128,256]{2,1,0:T(8,128)(2,1)S(1)}, bf16[6,128,256]{2,1,0:T(8,128)(2,1)S(1)}, u32[]{:S(2)}, u32[]{:S(2)}) %collective-permute-start.8) | collective-permute-done | bytes 393248 | tf_op jit(solution)/shard_map/ppermute | solution.py:25
  192.6 4.6 %collective-permute-start.10 = (bf16[24,6,256]{2,1,0:T(8,128)(2,1)S(1)}, bf16[24,6,256]{2,1,0:T(8,128)(2,1)S(1)}, u32[]{:S(2)}, u32[]{:S(2)}) collective-permute-start(bf16[24,6,256]{2,1,0:T(8,128)(2,1)S(1)} %get-tuple-element.16), channel_id=1, source_target_pairs={{0,2},{1,3},{4,6},{5,7},{8,10},{9,11},{12,14},{13,15},{16,18},{17,... | collective-permute-start | bytes 221192 | tf_op jit(solution)/shard_map/ppermute | solution.py:25
  197.2 3.9 %fusion.17 = bf16[6,256,384]{1,2,0:T(8,128)(2,1)} fusion(bf16[32,6,8,384]{3,2,1,0:T(8,128)(2,1)} %bitcast.23, s32[256]{0:T(256)S(1)} %fusion.76, pred[256]{0:T(512)(128)(4,1)S(1)} %compare_or_fusion), kind=kOutput, calls=%fused_computation.30 | convolution fusion | flops 303759360 | bytes 2360576 | tf_op jit(solution)/shard_map/rn,trc->tnc/dot_general | solution.py:187
  201.1 2.9 %copy.58 = bf16[6,256,384]{2,0,1:T(8,128)(2,1)} copy(bf16[6,256,384]{1,2,0:T(8,128)(2,1)} %fusion.17) | data formatting | bytes 2359296 | tf_op jit(solution)/shard_map/convert_element_type | solution.py:189
  204.0 4.6 %all-to-all-start.4 = ((bf16[6,256,384]{2,0,1:T(8,128)(2,1)}), bf16[6,256,384]{2,0,1:T(8,128)(2,1)}, u32[]{:S(2)}, u32[]{:S(2)}) async-start(bf16[6,256,384]{2,0,1:T(8,128)(2,1)} %copy.58), calls=%async_computation.4 | async-start | bytes 3145728 | tf_op jit(solution)/shard_map/all_to_all | solution.py:190
  209.8 15.5 %shard_map.195 = bf16[12,128,256]{2,1,0:T(8,128)(2,1)S(1)} custom-call(bf16[24,140,256]{2,1,0:T(8,128)(2,1)S(1)} %pad_maximum_fusion.1.field_ref, f32[49,1,256]{2,1,0:T(1,128)S(1)} %bitcast_convert_fusion.taps_ref, f32[1,256]{1,0:T(1,128)S(1)} %get-tuple-element.33.gain_ref, bf16[256,1024]{1,0:T(8,128)(2,1)S(1)} %get-tuple-element.25.up_ref, ...), custom_call_target="tpu_custom_call" | custom-call | flops 4076863488 | bytes 4489216 | tf_op jit(solution)/shard_map/pallas_call | solution.py:304
  232.8 5.1 %add_convert_fusion = bf16[24,64,384]{2,1,0:T(8,128)(2,1)} fusion(f32[24,64,384]{2,1,0:T(8,128)S(1)} %get-tuple-element.5, f32[384]{0:T(512)S(1)} %get-tuple-element.2, f32[24,64]{1,0:T(8,128)S(1)} %add_rsqrt_fusion, f32[24,64]{1,0:T(8,128)S(1)} %broadcast_multiply_fusion, bf16[768,384]{1,0:T(8,128)(2,1)S(1)} %copy-done, bf16[384,768]{1,0:T(8,128)(2,1)} %param.28), kind=kOutput, calls=%fused_computation.13 | convolution fusion | flops 1826095104 | bytes 4732416 | tf_op jit(solution)/shard_map/dot_general | solution.py:372
  (116 shorter events, 50.6 us)
Async XLA Ops:
  0.6 232.2 %copy-start = (bf16[768,384]{1,0:T(8,128)(2,1)S(1)}, bf16[768,384]{1,0:T(8,128)(2,1)}, u32[]{:S(2)}) copy-start(bf16[768,384]{1,0:T(8,128)(2,1)} %param.29) | copy-start | bytes 1769476
  0.6 7.7 %copy-start.18 = (f32[2,384]{1,0:T(2,128)S(1)}, f32[2,384]{1,0:T(2,128)}, u32[]{:S(2)}) copy-start(f32[2,384]{1,0:T(2,128)} %param.27) | copy-start | bytes 9220
  0.7 7.7 %copy-start.15 = (bf16[32,384]{1,0:T(8,128)(2,1)S(1)}, bf16[32,384]{1,0:T(8,128)(2,1)}, u32[]{:S(2)}) copy-start(bf16[32,384]{1,0:T(8,128)(2,1)} %param.31) | copy-start | bytes 73732
  0.7 7.7 %copy-start.8 = (bf16[24,64,384]{2,1,0:T(8,128)(2,1)S(1)}, bf16[24,64,384]{2,1,0:T(8,128)(2,1)}, u32[]{:S(2)}) copy-start(bf16[24,64,384]{2,1,0:T(8,128)(2,1)} %param.19) | copy-start | bytes 3538948
  10.5 5.2 %copy-start.16 = (bf16[384,32]{0,1:T(8,128)(2,1)S(1)}, bf16[384,32]{0,1:T(8,128)(2,1)}, u32[]{:S(2)}) copy-start(bf16[384,32]{0,1:T(8,128)(2,1)} %param.30) | copy-start | bytes 73732
  12.0 5.4 %copy-start.20 = (f32[192]{0:T(256)S(1)}, f32[192]{0:T(256)}, u32[]{:S(2)}) copy-start(f32[192]{0:T(256)} %param.23) | copy-start | bytes 2308
  12.0 19.5 %all-to-all-start.1 = ((bf16[24,64,384]{2,1,0:T(8,128)(2,1)}), bf16[24,64,384]{2,1,0:T(8,128)(2,1)S(1)}, u32[]{:S(2)}, u32[]{:S(2)}) async-start(bf16[24,64,384]{2,1,0:T(8,128)(2,1)} %multiply_convert_fusion.4), calls=%async_computation.1 | async-start | bytes 2359296 | tf_op jit(solution)/shard_map/all_to_all | solution.py:171
  31.4 7.2 %all-to-all-start.5 = ((bf16[2,2,12288]{2,1,0:T(2,128)(2,1)}), bf16[2,2,12288]{2,1,0:T(2,128)(2,1)S(1)}, u32[]{:S(2)}, u32[]{:S(2)}) async-start(bf16[2,2,12288]{2,1,0:T(2,128)(2,1)} %reshape.195), calls=%async_computation.5 | async-start | bytes 196608 | tf_op jit(solution)/shard_map/all_to_all | solution.py:354
  36.8 7.0 %copy-start.21 = (f32[384]{0:T(512)S(1)}, f32[384]{0:T(512)}, u32[]{:S(2)}) copy-start(f32[384]{0:T(512)} %param.26) | copy-start | bytes 4612
  38.7 78.0 %all-to-all-start.2 = ((bf16[6,256,384]{2,0,1:T(8,128)(2,1)}), bf16[6,256,384]{2,0,1:T(8,128)(2,1)}, u32[]{:S(2)}, u32[]{:S(2)}) async-start(bf16[6,256,384]{2,0,1:T(8,128)(2,1)} %copy.50), calls=%async_computation.2 | async-start | bytes 3145728 | tf_op jit(solution)/shard_map/all_to_all | solution.py:175
  43.8 8.0 %copy-start.5 = (bf16[12,128,256]{2,1,0:T(8,128)(2,1)S(1)}, bf16[12,128,256]{2,1,0:T(8,128)(2,1)}, u32[]{:S(2)}) copy-start(bf16[12,128,256]{2,1,0:T(8,128)(2,1)} %param.20) | copy-start | bytes 2359300
  43.8 8.0 %copy-start.17 = (bf16[32,256]{1,0:T(8,128)(2,1)S(1)}, bf16[32,256]{1,0:T(8,128)(2,1)}, u32[]{:S(2)}) copy-start(bf16[32,256]{1,0:T(8,128)(2,1)} %param.33) | copy-start | bytes 49156
  50.0 13.1 %collective-permute-start = (bf16[1,192,192]{2,1,0:T(8,128)(2,1)}, bf16[1,192,192]{2,1,0:T(8,128)(2,1)}, u32[]{:S(2)}, u32[]{:S(2)}) collective-permute-start(bf16[1,192,192]{2,1,0:T(8,128)(2,1)} %slice.96), channel_id=1, source_target_pairs={{9,8},{10,9},{11,10},{12,11},{13,12},{14,13},{15,14},{8,15},{25,24... | collective-permute-start | bytes 221192 | tf_op jit(solution)/shard_map/ppermute | solution.py:142
  53.3 94.9 %collective-permute-start.5 = (bf16[6,128,256]{2,1,0:T(8,128)(2,1)}, bf16[6,128,256]{2,1,0:T(8,128)(2,1)S(1)}, u32[]{:S(2)}, u32[]{:S(2)}) collective-permute-start(bf16[6,128,256]{2,1,0:T(8,128)(2,1)} %get-tuple-element.30), channel_id=1, source_target_pairs={{1,0},{4,1},{5,4},{8,5},{9,8},{12,9},{13,12},{16,13},{17,16},{20,1... | collective-permute-start | bytes 1179656 | tf_op jit(solution)/shard_map/ppermute | solution.py:28
  55.4 92.8 %collective-permute-start.4 = (bf16[6,128,256]{2,1,0:T(8,128)(2,1)}, bf16[6,128,256]{2,1,0:T(8,128)(2,1)}, u32[]{:S(2)}, u32[]{:S(2)}) collective-permute-start(bf16[6,128,256]{2,1,0:T(8,128)(2,1)} %get-tuple-element.29), channel_id=1, source_target_pairs={{0,1},{1,4},{4,5},{5,8},{8,9},{9,12},{12,13},{13,16},{16,17},{17,2... | collective-permute-start | bytes 1179656 | tf_op jit(solution)/shard_map/ppermute | solution.py:25
  67.5 39.4 %collective-permute-start.3 = (bf16[4,192,192]{2,1,0:T(8,128)(2,1)}, bf16[4,192,192]{2,1,0:T(8,128)(2,1)}, u32[]{:S(2)}, u32[]{:S(2)}) collective-permute-start(bf16[4,192,192]{2,1,0:T(8,128)(2,1)} %get-tuple-element.21), channel_id=1, source_target_pairs={{0,31},{15,16},{16,15},{31,0},{1,30},{14,17},{17,14},{30,1},{2,29}... | collective-permute-start | bytes 884744 | tf_op jit(solution)/shard_map/ppermute | solution.py:152
  70.4 36.5 %collective-permute-start.2 = (bf16[4,192,192]{2,1,0:T(8,128)(2,1)}, bf16[4,192,192]{2,1,0:T(8,128)(2,1)}, u32[]{:S(2)}, u32[]{:S(2)}) collective-permute-start(bf16[4,192,192]{2,1,0:T(8,128)(2,1)} %get-tuple-element.22), channel_id=1, source_target_pairs={{0,15},{15,0},{16,31},{31,16},{1,14},{14,1},{17,30},{30,17},{2,13}... | collective-permute-start | bytes 884744 | tf_op jit(solution)/shard_map/ppermute | solution.py:152
  71.4 41.1 %collective-permute-start.1 = (bf16[4,192,192]{2,1,0:T(8,128)(2,1)}, bf16[4,192,192]{2,1,0:T(8,128)(2,1)}, u32[]{:S(2)}, u32[]{:S(2)}) collective-permute-start(bf16[4,192,192]{2,1,0:T(8,128)(2,1)} %get-tuple-element.20), channel_id=1, source_target_pairs={{0,16},{15,31},{16,0},{31,15},{1,17},{14,30},{17,1},{30,14},{2,18}... | collective-permute-start | bytes 884744 | tf_op jit(solution)/shard_map/ppermute | solution.py:152
  130.8 15.2 %copy-start.13 = (bf16[2,7,7,256]{3,0,2,1:T(2,128)(2,1)S(1)}, bf16[2,7,7,256]{3,0,2,1:T(2,128)(2,1)}, u32[]{:S(2)}) copy-start(bf16[2,7,7,256]{3,0,2,1:T(2,128)(2,1)} %param.34) | copy-start | bytes 150532
  134.5 62.7 %all-to-all-start.3 = ((bf16[192,8,384]{2,1,0:T(8,128)(2,1)}), bf16[192,8,384]{2,1,0:T(8,128)(2,1)}, u32[]{:S(2)}, u32[]{:S(2)}) async-start(bf16[192,8,384]{2,1,0:T(8,128)(2,1)} %bitcast.22.after_ref), calls=%async_computation.3 | async-start | bytes 2359296 | tf_op jit(solution)/shard_map/all_to_all | solution.py:186
  146.0 9.2 %copy-start.19 = (f32[2,256]{1,0:T(2,128)S(1)}, f32[2,256]{1,0:T(2,128)}, u32[]{:S(2)}) copy-start(f32[2,256]{1,0:T(2,128)} %param.35) | copy-start | bytes 6148
  148.2 12.0 %copy-start.1 = (bf16[256,1024]{1,0:T(8,128)(2,1)S(1)}, bf16[256,1024]{1,0:T(8,128)(2,1)}, u32[]{:S(2)}) copy-start(bf16[256,1024]{1,0:T(8,128)(2,1)} %get-tuple-element.26.up_ref) | copy-start | bytes 1572868
  149.1 9.0 %collective-permute-start.7 = (bf16[24,6,256]{2,1,0:T(8,128)(2,1)S(1)}, bf16[24,6,256]{2,1,0:T(8,128)(2,1)S(1)}, u32[]{:S(2)}, u32[]{:S(2)}) collective-permute-start(bf16[24,6,256]{2,1,0:T(8,128)(2,1)S(1)} %get-tuple-element.19), channel_id=1, source_target_pairs={{2,0},{3,1},{6,4},{7,5},{10,8},{11,9},{14,12},{15,13},{18,16},{19,... | collective-permute-start | bytes 221192 | tf_op jit(solution)/shard_map/ppermute | solution.py:28
  150.4 7.7 %collective-permute-start.6 = (bf16[24,6,256]{2,1,0:T(8,128)(2,1)S(1)}, bf16[24,6,256]{2,1,0:T(8,128)(2,1)S(1)}, u32[]{:S(2)}, u32[]{:S(2)}) collective-permute-start(bf16[24,6,256]{2,1,0:T(8,128)(2,1)S(1)} %get-tuple-element.18), channel_id=1, source_target_pairs={{0,2},{1,3},{4,6},{5,7},{8,10},{9,11},{12,14},{13,15},{16,18},{17,... | collective-permute-start | bytes 221192 | tf_op jit(solution)/shard_map/ppermute | solution.py:25
  175.8 11.7 %collective-permute-start.9 = (bf16[6,128,256]{2,1,0:T(8,128)(2,1)S(1)}, bf16[6,128,256]{2,1,0:T(8,128)(2,1)S(1)}, u32[]{:S(2)}, u32[]{:S(2)}) collective-permute-start(bf16[6,128,256]{2,1,0:T(8,128)(2,1)S(1)} %get-tuple-element.28), channel_id=1, source_target_pairs={{1,0},{4,1},{5,4},{8,5},{9,8},{12,9},{13,12},{16,13},{17,16},{20,1... | collective-permute-start | bytes 1179656 | tf_op jit(solution)/shard_map/ppermute | solution.py:28
  178.0 13.3 %collective-permute-start.8 = (bf16[6,128,256]{2,1,0:T(8,128)(2,1)S(1)}, bf16[6,128,256]{2,1,0:T(8,128)(2,1)S(1)}, u32[]{:S(2)}, u32[]{:S(2)}) collective-permute-start(bf16[6,128,256]{2,1,0:T(8,128)(2,1)S(1)} %get-tuple-element.27), channel_id=1, source_target_pairs={{0,1},{1,4},{4,5},{5,8},{8,9},{9,12},{12,13},{13,16},{16,17},{17,2... | collective-permute-start | bytes 1179656 | tf_op jit(solution)/shard_map/ppermute | solution.py:25
  191.3 17.3 %collective-permute-start.11 = (bf16[24,6,256]{2,1,0:T(8,128)(2,1)S(1)}, bf16[24,6,256]{2,1,0:T(8,128)(2,1)S(1)}, u32[]{:S(2)}, u32[]{:S(2)}) collective-permute-start(bf16[24,6,256]{2,1,0:T(8,128)(2,1)S(1)} %get-tuple-element.17), channel_id=1, source_target_pairs={{2,0},{3,1},{6,4},{7,5},{10,8},{11,9},{14,12},{15,13},{18,16},{19,... | collective-permute-start | bytes 221192 | tf_op jit(solution)/shard_map/ppermute | solution.py:28
  192.6 16.0 %collective-permute-start.10 = (bf16[24,6,256]{2,1,0:T(8,128)(2,1)S(1)}, bf16[24,6,256]{2,1,0:T(8,128)(2,1)S(1)}, u32[]{:S(2)}, u32[]{:S(2)}) collective-permute-start(bf16[24,6,256]{2,1,0:T(8,128)(2,1)S(1)} %get-tuple-element.16), channel_id=1, source_target_pairs={{0,2},{1,3},{4,6},{5,7},{8,10},{9,11},{12,14},{13,15},{16,18},{17,... | collective-permute-start | bytes 221192 | tf_op jit(solution)/shard_map/ppermute | solution.py:25
  201.1 7.5 %copy-start.14 = (s32[12,128]{1,0:T(8,128)S(1)}, s32[12,128]{1,0:T(8,128)}, u32[]{:S(2)}) copy-start(s32[12,128]{1,0:T(8,128)} %param.21) | copy-start | bytes 18436
  204.0 24.5 %all-to-all-start.4 = ((bf16[6,256,384]{2,0,1:T(8,128)(2,1)}), bf16[6,256,384]{2,0,1:T(8,128)(2,1)}, u32[]{:S(2)}, u32[]{:S(2)}) async-start(bf16[6,256,384]{2,0,1:T(8,128)(2,1)} %copy.58), calls=%async_computation.4 | async-start | bytes 3145728 | tf_op jit(solution)/shard_map/all_to_all | solution.py:190
  209.8 15.5 %copy-start.6 = (bf16[12,128,256]{2,1,0:T(8,128)(2,1)S(1)}, bf16[12,128,256]{2,1,0:T(8,128)(2,1)}, u32[]{:S(2)}) copy-start(bf16[12,128,256]{2,1,0:T(8,128)(2,1)} %param.20) | copy-start | bytes 2359300
  230.3 1.7 copy-start.4
  (7 other events, 9.4 us)
